TPU v7x, 32 devices: a whole 2x2x4 slice. The times are simulated.
32 devices in a mesh: dp: 8 (over z, x), tensor: 4 (over y, core).
Axes of the slice: x: 2, y: 2, z: 4, core: 2. Of those that a mesh axis runs over, the one named last changes fastest.
Arguments:
- decoder_in: bfloat16 [8, 128, 768], P('dp'), may hold values from -6 to 6
- encoder_out: bfloat16 [8, 6144, 768], P('dp', 'tensor'), may hold values from -6 to 6
- out_grad: bfloat16 [8, 128, 768], P('dp'), may hold values from -6 to 6
- group_ids: int32 [8], P('dp'), may hold values from 0 to 3
- target_mask: int32 [8, 128], P('dp'), may hold values 0 or 1
- bucket_ids: int32 [128, 128], replicated, may hold values from 0 to 31
- gain_self: float32 [768], replicated, may hold values from 0.5 to 1.5
- gain_cross: float32 [768], replicated, may hold values from 0.5 to 1.5
- gain_ffn: float32 [768], replicated, may hold values from 0.5 to 1.5
- query_self: bfloat16 [768, 768], P(None, 'tensor'), may hold values from -0.0546875 to 0.0546875
- key_self: bfloat16 [768, 768], P(None, 'tensor'), may hold values from -0.21875 to 0.21875
- value_self: bfloat16 [768, 768], P(None, 'tensor'), may hold values from -0.21875 to 0.21875
- output_self: bfloat16 [768, 768], P('tensor'), may hold values from -0.75 to 0.75
- query_cross: bfloat16 [768, 768], P(None, 'tensor'), may hold values from -0.0546875 to 0.0546875
- key_cross: bfloat16 [768, 768], P(None, 'tensor'), may hold values from -0.21875 to 0.21875
- value_cross: bfloat16 [768, 768], P(None, 'tensor'), may hold values from -0.21875 to 0.21875
- output_cross: bfloat16 [768, 768], P('tensor'), may hold values from -2 to 2
- gate_weight: bfloat16 [768, 2048], P(None, 'tensor'), may hold values from -0.21875 to 0.21875
- up_weight: bfloat16 [768, 2048], P(None, 'tensor'), may hold values from -0.21875 to 0.21875
- down_weight: bfloat16 [2048, 768], P('tensor'), may hold values from -0.1875 to 0.1875
- position_bias: float32 [4, 32, 12], P(None, None, 'tensor'), may hold values from -4 to 4
Outputs:
- block_out: bfloat16 [8, 128, 768], P('dp')
- decoder_grad: bfloat16 [8, 128, 768], P('dp')
- encoder_grad: bfloat16 [8, 6144, 768], P('dp', 'tensor')
- grad_gain_self: float32 [768], replicated
- grad_gain_cross: float32 [768], replicated
- grad_gain_ffn: float32 [768], replicated
- grad_query_self: float32 [768, 768], P(None, 'tensor')
- grad_key_self: float32 [768, 768], P(None, 'tensor')
- grad_value_self: float32 [768, 768], P(None, 'tensor')
- grad_output_self: float32 [768, 768], P('tensor')
- grad_query_cross: float32 [768, 768], P(None, 'tensor')
- grad_key_cross: float32 [768, 768], P(None, 'tensor')
- grad_value_cross: float32 [768, 768], P(None, 'tensor')
- grad_output_cross: float32 [768, 768], P('tensor')
- grad_gate: float32 [768, 2048], P(None, 'tensor')
- grad_up: float32 [768, 2048], P(None, 'tensor')
- grad_down: float32 [2048, 768], P('tensor')
- grad_position: float32 [4, 32, 12], P(None, None, 'tensor')
All inputs are finite; a program needn't handle non-finite values. No bound on the sum of `target_mask` on one device may be relied on, other than what follows from the above.
Results may differ from a plain program's by a relative error of at most 0.039.
The roundings to bfloat16 on the way count: a program that leaves them out, or rounds other values in their place, can miss the bound.
Values may be sent and summed in bfloat16 or wider, within the bound.
A program may use at most 128 MiB of HBM per device.

v0:
```python
import jax
import jax.numpy as jnp
from jax import lax
from jax.sharding import PartitionSpec as P

DH = 64


EPS = 1e-06
NEG = -1000000000.0
HIGH = lax.Precision.HIGHEST


def merged(shard, axis, combine):
    everything = jax.tree.map(lambda part: lax.all_gather(part, axis), shard)
    leading = jax.tree.map(lambda part: part[0], everything)

    def turn(k, so_far):
        return combine(so_far, jax.tree.map(lambda part: part[k], everything))

    return lax.fori_loop(1, lax.axis_size(axis), turn, leading)


def rms_norm(values, gain):
    return values * lax.rsqrt(jnp.mean(values * values, axis=-1, keepdims=True) + EPS) * gain


def gated(gate_value, up_value):
    return jax.nn.gelu(gate_value, approximate=True) * up_value


def matmul(left, right):
    return jnp.dot(left, right, preferred_element_type=jnp.float32)


def matmul_left_t(left, right):
    return lax.dot_general(
        left, right, (((0,), (0,)), ((), ())), preferred_element_type=jnp.float32
    )


def matmul_right_t(left, right):
    return lax.dot_general(
        left, right, (((1,), (1,)), ((), ())), preferred_element_type=jnp.float32
    )


def score_block(query_heads, key_heads, bias):
    return (
        jnp.einsum("bihd,bjhd->bhij", query_heads, key_heads, preferred_element_type=jnp.float32)
        + bias
    )


def combine_parts(first, second):
    top = jnp.maximum(first[0], second[0])
    return (top, first[1] * jnp.exp(first[0] - top) + second[1] * jnp.exp(second[0] - top))


def attend_forward(query_heads, key_heads, value_heads, bias):
    scores = score_block(query_heads, key_heads, bias)
    row_max = jnp.max(scores, axis=-1, keepdims=True)
    log_total = row_max + jnp.log(jnp.sum(jnp.exp(scores - row_max), axis=-1, keepdims=True))
    weights_low = jnp.exp(scores - log_total).astype(jnp.bfloat16)
    mixture = jnp.einsum(
        "bhij,bjhd->bihd", weights_low, value_heads, preferred_element_type=jnp.float32
    )
    return (mixture.astype(jnp.bfloat16), log_total)


def attend_backward(query_heads, key_heads, value_heads, bias, log_total, mixture_grad):
    scores = score_block(query_heads, key_heads, bias)
    probabilities = jnp.exp(scores - log_total)
    weights_low = probabilities.astype(jnp.bfloat16)
    prob_grad = jnp.einsum(
        "bihd,bjhd->bhij", mixture_grad, value_heads, preferred_element_type=jnp.float32
    )
    inner = jnp.sum(probabilities * prob_grad, axis=-1, keepdims=True)
    score_grad = (probabilities * (prob_grad - inner)).astype(jnp.bfloat16)
    value_grad = jnp.einsum(
        "bhij,bihd->bjhd", weights_low, mixture_grad, preferred_element_type=jnp.float32
    ).astype(jnp.bfloat16)
    key_grad = jnp.einsum(
        "bhij,bihd->bjhd", score_grad, query_heads, preferred_element_type=jnp.float32
    ).astype(jnp.bfloat16)
    query_grad = jnp.einsum(
        "bhij,bjhd->bihd", score_grad, key_heads, preferred_element_type=jnp.float32
    ).astype(jnp.bfloat16)
    return (query_grad, key_grad, value_grad, score_grad)


def shards(
    decoder_in,
    encoder_out,
    out_grad,
    group_ids,
    target_mask,
    bucket_ids,
    gain_self,
    gain_cross,
    gain_ffn,
    query_self,
    key_self,
    value_self,
    output_self,
    query_cross,
    key_cross,
    value_cross,
    output_cross,
    gate_weight,
    up_weight,
    down_weight,
    position_bias,
):
    query_count, target_len, model_width = decoder_in.shape
    local_heads = query_self.shape[1] // DH
    rows_total = query_count * target_len
    group_count = position_bias.shape[0]
    bucket_count = position_bias.shape[1]
    own_rows = encoder_out.shape[1]

    def to_heads(values, row_count):
        return values.reshape(query_count, row_count, local_heads, DH)

    flat_in = decoder_in.reshape(rows_total, model_width).astype(jnp.float32)
    positions = jnp.arange(target_len)
    causal = positions[None, :] <= positions[:, None]
    diagonal = positions[None, :] == positions[:, None]
    allowed = causal[None] & ((target_mask[:, None, :] == 1) | diagonal[None])
    group_hot = (group_ids[:, None] == jnp.arange(group_count)[None, :]).astype(jnp.float32)
    bucket_hot = (jnp.arange(bucket_count)[:, None] == bucket_ids.reshape(-1)[None, :]).astype(
        jnp.float32
    )
    group_table = jnp.einsum("bg,gkh->bkh", group_hot, position_bias, precision=HIGH)
    spread_bias = jnp.einsum("kp,bkh->bhp", bucket_hot, group_table, precision=HIGH)
    spread_bias = spread_bias.reshape(query_count, local_heads, target_len, target_len)
    self_bias = jnp.where(allowed[:, None], spread_bias, NEG)
    self_input = rms_norm(flat_in, gain_self).astype(jnp.bfloat16)
    self_query = to_heads(matmul(self_input, query_self).astype(jnp.bfloat16), target_len)
    self_key = to_heads(matmul(self_input, key_self).astype(jnp.bfloat16), target_len)
    self_value = to_heads(matmul(self_input, value_self).astype(jnp.bfloat16), target_len)
    self_mix, self_total = attend_forward(self_query, self_key, self_value, self_bias)
    self_flat = self_mix.reshape(rows_total, local_heads * DH)
    after_self = flat_in + lax.psum(matmul(self_flat, output_self), "tensor")
    cross_input = rms_norm(after_self, gain_cross).astype(jnp.bfloat16)
    query_flat = matmul(cross_input, query_cross).astype(jnp.bfloat16)
    key_whole, value_whole, query_whole, output_whole = (
        lax.all_gather(key_cross, "tensor", axis=1, tiled=True),
        lax.all_gather(value_cross, "tensor", axis=1, tiled=True),
        lax.all_gather(query_flat, "tensor", axis=1, tiled=True),
        lax.all_gather(output_cross, "tensor", axis=0, tiled=True),
    )
    head_total = key_whole.shape[1] // DH
    own_key = (
        jnp.einsum("bsd,de->bse", encoder_out, key_whole, preferred_element_type=jnp.float32)
        .astype(jnp.bfloat16)
        .reshape(query_count, own_rows, head_total, DH)
    )
    own_value = (
        jnp.einsum("bsd,de->bse", encoder_out, value_whole, preferred_element_type=jnp.float32)
        .astype(jnp.bfloat16)
        .reshape(query_count, own_rows, head_total, DH)
    )
    query_all = query_whole.reshape(query_count, target_len, head_total, DH)
    own_scores = score_block(query_all, own_key, 0.0)
    own_max = jnp.max(own_scores, axis=-1, keepdims=True)
    own_sum = jnp.sum(jnp.exp(own_scores - own_max), axis=-1, keepdims=True)
    top_all, sum_all = merged((own_max, own_sum), "tensor", combine_parts)
    cross_total = top_all + jnp.log(sum_all)
    own_weights = jnp.exp(own_scores - cross_total).astype(jnp.bfloat16)
    partial_mix = jnp.einsum(
        "bhij,bjhd->bihd", own_weights, own_value, preferred_element_type=jnp.float32
    )
    cross_mix = lax.psum_scatter(
        partial_mix.astype(jnp.bfloat16), "tensor", scatter_dimension=2, tiled=True
    )
    cross_flat = cross_mix.reshape(rows_total, local_heads * DH)
    after_cross = after_self + lax.psum(
        matmul(cross_flat, output_cross).astype(jnp.bfloat16), "tensor"
    ).astype(jnp.float32)
    ffn_input = rms_norm(after_cross, gain_ffn).astype(jnp.bfloat16)
    gate_value = matmul(ffn_input, gate_weight)
    up_value = matmul(ffn_input, up_weight)
    hidden_low = gated(gate_value, up_value).astype(jnp.bfloat16)
    ffn_result = lax.psum(matmul(hidden_low, down_weight).astype(jnp.bfloat16), "tensor").astype(
        jnp.float32
    )
    block_out = (
        (after_cross + ffn_result)
        .astype(jnp.bfloat16)
        .reshape(query_count, target_len, model_width)
    )
    out_low = out_grad.reshape(rows_total, model_width)
    residual_grad = out_low.astype(jnp.float32)
    grad_down = matmul_left_t(hidden_low, out_low)
    hidden_grad = matmul_right_t(out_low, down_weight).astype(jnp.bfloat16)
    unused_gate, gated_pull = jax.vjp(gated, gate_value, up_value)
    gate_grad, up_grad = gated_pull(hidden_grad.astype(jnp.float32))
    gate_low = gate_grad.astype(jnp.bfloat16)
    up_low = up_grad.astype(jnp.bfloat16)
    grad_gate = matmul_left_t(ffn_input, gate_low)
    grad_up = matmul_left_t(ffn_input, up_low)
    ffn_in_grad = lax.psum(
        (matmul_right_t(gate_low, gate_weight) + matmul_right_t(up_low, up_weight)).astype(
            jnp.bfloat16
        ),
        "tensor",
    ).astype(jnp.float32)
    unused_ffn, ffn_pull = jax.vjp(rms_norm, after_cross, gain_ffn)
    ffn_norm_grad, grad_gain_ffn = ffn_pull(ffn_in_grad)
    cross_residual = residual_grad + ffn_norm_grad
    cross_low = cross_residual.astype(jnp.bfloat16)
    grad_output_cross = matmul_left_t(cross_flat, cross_low)
    mix_grad_all = (
        matmul_right_t(cross_low, output_whole)
        .astype(jnp.bfloat16)
        .reshape(query_count, target_len, head_total, DH)
    )
    back_scores = score_block(query_all, own_key, 0.0)
    probabilities = jnp.exp(back_scores - cross_total)
    back_weights = probabilities.astype(jnp.bfloat16)
    prob_grad = jnp.einsum(
        "bihd,bjhd->bhij", mix_grad_all, own_value, preferred_element_type=jnp.float32
    )
    inner = lax.psum(jnp.sum(probabilities * prob_grad, axis=-1, keepdims=True), "tensor")
    score_grad_cross = (probabilities * (prob_grad - inner)).astype(jnp.bfloat16)
    ck_flat = (
        jnp.einsum(
            "bhij,bihd->bjhd", score_grad_cross, query_all, preferred_element_type=jnp.float32
        )
        .astype(jnp.bfloat16)
        .reshape(query_count, own_rows, head_total * DH)
    )
    cv_flat = (
        jnp.einsum(
            "bhij,bihd->bjhd", back_weights, mix_grad_all, preferred_element_type=jnp.float32
        )
        .astype(jnp.bfloat16)
        .reshape(query_count, own_rows, head_total * DH)
    )
    query_part = jnp.einsum(
        "bhij,bjhd->bihd", score_grad_cross, own_key, preferred_element_type=jnp.float32
    ).reshape(rows_total, head_total, DH)
    encoder_term = jnp.einsum("bse,de->bsd", ck_flat, key_whole, preferred_element_type=jnp.float32)
    encoder_term = encoder_term + jnp.einsum(
        "bse,de->bsd", cv_flat, value_whole, preferred_element_type=jnp.float32
    )
    encoder_grad = encoder_term.astype(jnp.bfloat16)
    key_part = jnp.einsum(
        "bsd,bse->de", encoder_out, ck_flat, preferred_element_type=jnp.float32
    ).reshape(model_width, head_total, DH)
    value_part = jnp.einsum(
        "bsd,bse->de", encoder_out, cv_flat, preferred_element_type=jnp.float32
    ).reshape(model_width, head_total, DH)
    query_sum, key_sum, value_sum = (
        lax.psum_scatter(
            query_part.astype(jnp.bfloat16), "tensor", scatter_dimension=1, tiled=True
        ).astype(jnp.float32),
        lax.psum_scatter(
            key_part.astype(jnp.bfloat16), "tensor", scatter_dimension=1, tiled=True
        ).astype(jnp.float32),
        lax.psum_scatter(
            value_part.astype(jnp.bfloat16), "tensor", scatter_dimension=1, tiled=True
        ).astype(jnp.float32),
    )
    cq_flat = query_sum.astype(jnp.bfloat16).reshape(rows_total, local_heads * DH)
    grad_key_cross = key_sum.reshape(model_width, local_heads * DH)
    grad_value_cross = value_sum.reshape(model_width, local_heads * DH)
    grad_query_cross = matmul_left_t(cross_input, cq_flat)
    cross_in_grad = lax.psum(
        matmul_right_t(cq_flat, query_cross).astype(jnp.bfloat16), "tensor"
    ).astype(jnp.float32)
    unused_cross, cross_pull = jax.vjp(rms_norm, after_self, gain_cross)
    cross_norm_grad, grad_gain_cross = cross_pull(cross_in_grad)
    self_residual = cross_residual + cross_norm_grad
    self_low = self_residual.astype(jnp.bfloat16)
    grad_output_self = matmul_left_t(self_flat, self_low)
    self_mix_grad = to_heads(matmul_right_t(self_low, output_self).astype(jnp.bfloat16), target_len)
    sq_grad, sk_grad, sv_grad, score_grad = attend_backward(
        self_query, self_key, self_value, self_bias, self_total, self_mix_grad
    )
    table_grad = jnp.einsum(
        "bhp,kp->bkh",
        score_grad.reshape(query_count, local_heads, target_len * target_len),
        bucket_hot.astype(jnp.bfloat16),
        preferred_element_type=jnp.float32,
    )
    grad_position = jnp.einsum("bg,bkh->gkh", group_hot, table_grad, precision=HIGH)
    sq_flat = sq_grad.reshape(rows_total, local_heads * DH)
    sk_flat = sk_grad.reshape(rows_total, local_heads * DH)
    sv_flat = sv_grad.reshape(rows_total, local_heads * DH)
    grad_query_self = matmul_left_t(self_input, sq_flat)
    grad_key_self = matmul_left_t(self_input, sk_flat)
    grad_value_self = matmul_left_t(self_input, sv_flat)
    self_term = (
        matmul_right_t(sq_flat, query_self)
        + matmul_right_t(sk_flat, key_self)
        + matmul_right_t(sv_flat, value_self)
    )
    self_in_grad = lax.psum(self_term.astype(jnp.bfloat16), "tensor").astype(jnp.float32)
    unused_self, self_pull = jax.vjp(rms_norm, flat_in, gain_self)
    self_norm_grad, grad_gain_self = self_pull(self_in_grad)
    decoder_grad = (
        (self_residual + self_norm_grad)
        .astype(jnp.bfloat16)
        .reshape(query_count, target_len, model_width)
    )
    summed = lax.psum(
        (
            grad_gain_self,
            grad_gain_cross,
            grad_gain_ffn,
            grad_query_self,
            grad_key_self,
            grad_value_self,
            grad_output_self,
            grad_query_cross,
            grad_key_cross,
            grad_value_cross,
            grad_output_cross,
            grad_gate,
            grad_up,
            grad_down,
            grad_position,
        ),
        "dp",
    )
    return (block_out, decoder_grad, encoder_grad) + tuple(summed)


def solution(mesh):
    placed = (
        P("dp", None, None),
        P("dp", "tensor", None),
        P("dp", None, None),
        P("dp"),
        P("dp", None),
        P(),
        P(),
        P(),
        P(),
        P(None, "tensor"),
        P(None, "tensor"),
        P(None, "tensor"),
        P("tensor", None),
        P(None, "tensor"),
        P(None, "tensor"),
        P(None, "tensor"),
        P("tensor", None),
        P(None, "tensor"),
        P(None, "tensor"),
        P("tensor", None),
        P(None, None, "tensor"),
    )
    return jax.shard_map(
        shards,
        mesh=mesh,
        in_specs=placed,
        out_specs=(
            P("dp", None, None),
            P("dp", None, None),
            P("dp", "tensor", None),
            P(),
            P(),
            P(),
            P(None, "tensor"),
            P(None, "tensor"),
            P(None, "tensor"),
            P("tensor", None),
            P(None, "tensor"),
            P(None, "tensor"),
            P(None, "tensor"),
            P("tensor", None),
            P(None, "tensor"),
            P(None, "tensor"),
            P("tensor", None),
            P(None, None, "tensor"),
        ),
        check_vma=False,
    )
```

profile of v0, /device:TPU:0, one launch (start us, length us, event | category | flops | bytes accessed | tf_op | source)
XLA Modules:
  0.0 730.7 jit_solution(12198469555481382830)
XLA Ops:
  20.6 33.9 %all-reduce.10.cloned.1.call-done = f32[128,768]{1,0:T(8,128)} async-done(((f32[128,768]{1,0:T(8,128)}), f32[128,768]{1,0:T(8,128)}) %all-reduce.10.cloned.1.call-update) | async-done | bytes 393232 | tf_op jit(solution)/shard_map/psum | solution.py:144
  56.2 5.6 all_gather.19
  61.8 11.9 %all-gather.10.cloned.1.call-done = bf16[768,768]{0,1:T(8,128)(2,1)} async-done(((bf16[768,192]{0,1:T(8,128)(2,1)}), bf16[768,768]{0,1:T(8,128)(2,1)}) %all-gather.10.cloned.1.call-update) | async-done | bytes 1179664 | tf_op jit(solution)/shard_map/all_gather | solution.py:148
  73.7 3.3 convolution_convert_fusion.2
  78.6 5.2 all-gather.2
  85.2 5.3 all-gather.3
  93.0 3.4 convolution_convert_fusion.3
  97.9 2.5 fusion.33
  100.5 19.8 %reduce-scatter.5.cloned.1.call-done = bf16[1,128,3,64]{1,3,2,0:T(8,128)(2,1)} async-done(((bf16[1,128,12,64]{1,3,2,0:T(8,128)(2,1)}), bf16[1,128,3,64]{1,3,2,0:T(8,128)(2,1)}) %reduce-scatter.5.cloned.1.call-update) | async-done | bytes 49168 | tf_op jit(solution)/shard_map/reduce_scatter | solution.py:174
  122.3 32.6 %all-reduce.12.cloned.1.call-done = bf16[128,768]{1,0:T(8,128)(2,1)} async-done(((bf16[128,768]{1,0:T(8,128)(2,1)}), bf16[128,768]{1,0:T(8,128)(2,1)}) %all-reduce.12.cloned.1.call-update) | async-done | bytes 196624 | tf_op jit(solution)/shard_map/psum | solution.py:178
  163.9 31.0 %all-reduce.14.cloned.1.call-done = bf16[128,768]{1,0:T(8,128)(2,1)} async-done(((bf16[128,768]{1,0:T(8,128)(2,1)}), bf16[128,768]{1,0:T(8,128)(2,1)}) %all-reduce.14.cloned.1.call-update) | async-done | bytes 196624 | tf_op jit(solution)/shard_map/psum | solution.py:203
  199.2 14.9 %all-gather.12.cloned.1.call-done = bf16[768,768]{1,0:T(8,128)(2,1)} async-done(((bf16[192,768]{1,0:T(8,128)(2,1)}), bf16[768,768]{1,0:T(8,128)(2,1)}) %all-gather.12.cloned.1.call-update) | async-done | bytes 1179664 | tf_op jit(solution)/shard_map/all_gather | solution.py:151
  214.1 2.6 convolution_convert_fusion.6
  218.5 10.5 %multiply_reduce_fusion = (f32[12,128]{1,0:T(8,128)}, f32[12,128,1536]{2,1,0:T(8,128)}) fusion(f32[12,128,1536]{2,1,0:T(8,128)} %copy-done.1, f32[12,128]{1,0:T(8,128)S(1)} %bitcast.273, bf16[128,12,64]{0,2,1:T(8,128)(2,1)} %bitcast.258, bf16[1536,12,64]{0,2,1:T(8,128)(2,1)} %bitcast.253), kind=kOutput, calls=%fused_computation.6 | convolution fusion | flops 309066240 | bytes 21442560 | tf_op jit(solution)/shard_map/bihd,bjhd->bhij/dot_general | solution.py:222
  229.0 6.7 psum.158
  235.7 7.6 %multiply_convert_fusion = bf16[12,128,1536]{2,1,0:T(8,128)(2,1)S(1)} fusion(f32[12,128,1536]{2,1,0:T(8,128)} %get-tuple-element.210, f32[12,128,1536]{2,1,0:T(8,128)} %copy-done.1, f32[12,128]{1,0:T(8,128)} %psum.158, f32[12,128]{1,0:T(8,128)S(1)} %bitcast.274), kind=kLoop, calls=%fused_computation.5 | loop fusion | flops 9437184 | bytes 23605248 | tf_op jit(solution)/shard_map/convert_element_type | solution.py:226
  245.4 2.4 fusion.31
  247.9 4.6 convolution_convert_fusion.1
  252.6 16.2 %reduce-scatter.7.cloned.1.call-done = bf16[128,3,64]{0,2,1:T(8,128)(2,1)} async-done(((bf16[128,12,64]{0,2,1:T(8,128)(2,1)}), bf16[128,3,64]{0,2,1:T(8,128)(2,1)}) %reduce-scatter.7.cloned.1.call-update) | async-done | bytes 49168 | tf_op jit(solution)/shard_map/reduce_scatter | solution.py:256
  270.8 4.7 fusion.20
  275.6 2.2 convolution_convert_fusion.8
  277.8 2.5 fusion.118
  284.4 5.5 convolution_convert_fusion
  291.4 3.0 fusion.17
  296.7 6.9 all-reduce.16.cloned.1.call-done
  314.8 17.0 %reduce-scatter.9.cloned.1.call-done = bf16[768,3,64]{0,2,1:T(8,128)(2,1)} async-done(((bf16[768,12,64]{0,2,1:T(8,128)(2,1)}), bf16[768,3,64]{0,2,1:T(8,128)(2,1)}) %reduce-scatter.9.cloned.1.call-update) | async-done | bytes 294928 | tf_op jit(solution)/shard_map/reduce_scatter | solution.py:259
  333.6 26.7 %reduce-scatter.11.cloned.1.call-done = bf16[768,3,64]{0,2,1:T(8,128)(2,1)} async-done(((bf16[768,12,64]{0,2,1:T(8,128)(2,1)}), bf16[768,3,64]{0,2,1:T(8,128)(2,1)}) %reduce-scatter.11.cloned.1.call-update) | async-done | bytes 294928 | tf_op jit(solution)/shard_map/reduce_scatter | solution.py:262
  362.6 4.2 fusion.117
  366.8 3.5 fusion.3
  372.4 23.4 %all-reduce.20.cloned.1.call-done = (bf16[128,768]{1,0:T(8,128)(2,1)}, bf16[128,768]{1,0:T(8,128)(2,1)}) async-done(((bf16[128,768]{1,0:T(8,128)(2,1)}, bf16[128,768]{1,0:T(8,128)(2,1)}), (bf16[128,768]{1,0:T(8,128)(2,1)}, bf16[128,768]{1,0:T(8,128)(2,1)})) %all-reduce.20.cloned.1.call-update) | async-done | bytes 393232 | tf_op jit(solution)/shard_map/psum | solution.py:185
  396.9 38.7 %all-reduce = (f32[768]{0:T(1024)}, f32[768]{0:T(1024)}, f32[768]{0:T(1024)}, f32[4,32,3]{1,0,2:T(4,128)}) all-reduce(f32[768]{0:T(1024)S(1)} %get-tuple-element.167, f32[768]{0:T(1024)S(1)} %get-tuple-element.165, f32[768]{0:T(1024)S(1)} %copy-done.56, ...), channel_id=1, replica_groups=mesh['dp'=8,'tensor'=4] {'dp'}, use_global_device_ids=true, to_apply=%region_24.25 | all-reduce | flops 2688 | bytes 21504 | tf_op jit(solution)/shard_map/psum | solution.py:308
  438.3 272.7 %all-reduce.18.cloned.1.call-done = (f32[768,192]{0,1:T(8,128)}, f32[768,192]{0,1:T(8,128)}, f32[768,192]{0,1:T(8,128)}, f32[192,768]{1,0:T(8,128)}, f32[768,192...) async-done(((f32[768,192]{0,1:T(8,128)}, ...) | async-done | bytes 9437200 | tf_op jit(solution)/shard_map/psum | solution.py:308
  (248 shorter events, 84.3 us)
Async XLA Ops:
  7.2 66.5 %copy-start = (bf16[1,1536,768]{2,1,0:T(8,128)(2,1)S(1)}, bf16[1,1536,768]{2,1,0:T(8,128)(2,1)}, u32[]{:S(2)}) copy-start(bf16[1,1536,768]{2,1,0:T(8,128)(2,1)} %param.24) | copy-start | bytes 7077892
  7.2 9.0 %copy-start.4 = (bf16[1,128,768]{2,1,0:T(8,128)(2,1)S(1)}, bf16[1,128,768]{2,1,0:T(8,128)(2,1)}, u32[]{:S(2)}) copy-start(bf16[1,128,768]{2,1,0:T(8,128)(2,1)} %param.23) | copy-start | bytes 589828
  7.2 9.0 %copy-start.52 = (f32[768]{0:T(1024)S(1)}, f32[768]{0:T(1024)}, u32[]{:S(2)}) copy-start(f32[768]{0:T(1024)} %param.29) | copy-start | bytes 9220
  7.2 9.0 %copy-start.43 = (bf16[768,192]{0,1:T(8,128)(2,1)S(1)}, bf16[768,192]{0,1:T(8,128)(2,1)}, u32[]{:S(2)}) copy-start(bf16[768,192]{0,1:T(8,128)(2,1)} %param.33) | copy-start | bytes 884740
  7.2 10.8 %copy-start.26 = (bf16[192,768]{1,0:T(8,128)(2,1)S(1)}, bf16[192,768]{1,0:T(8,128)(2,1)}, u32[]{:S(2)}) copy-start(bf16[192,768]{1,0:T(8,128)(2,1)} %param.35) | copy-start | bytes 884740
  7.3 47.3 %all-reduce.10.cloned.1.call-start = ((), (), s32[]{:S(2)}) async-start(), calls=%async_computation.4 | async-start | bytes 786432 | tf_op jit(solution)/shard_map/psum | solution.py:144
  8.5 9.3 %copy-start.57 = (f32[128]{0:T(128)}, f32[128]{0:T(128)S(1)}, u32[]{:S(2)}) copy-start(f32[128]{0:T(128)S(1)} %fusion.96) | copy-start | bytes 1540
  14.8 40.9 %copy-start.46 = (bf16[128,192]{0,1:T(8,128)(2,1)}, bf16[128,192]{0,1:T(8,128)(2,1)S(1)}, u32[]{:S(2)}) copy-start(bf16[128,192]{0,1:T(8,128)(2,1)S(1)} %convolution_convert_fusion.18) | copy-start | bytes 147460
  14.8 40.9 %copy-start.25 = (bf16[768,192]{0,1:T(8,128)(2,1)S(1)}, bf16[768,192]{0,1:T(8,128)(2,1)}, u32[]{:S(2)}) copy-start(bf16[768,192]{0,1:T(8,128)(2,1)} %param.36) | copy-start | bytes 884740
  14.8 40.9 %copy-start.53 = (f32[768]{0:T(1024)S(1)}, f32[768]{0:T(1024)}, u32[]{:S(2)}) copy-start(f32[768]{0:T(1024)} %param.30) | copy-start | bytes 9220
  17.9 59.1 %copy-start.54 = (f32[3,128]{1,0:T(4,128)}, f32[3,128]{1,0:T(4,128)S(1)}, u32[]{:S(2)}) copy-start(f32[3,128]{1,0:T(4,128)S(1)} %log_add_fusion.1) | copy-start | bytes 4612
  18.1 58.9 %copy-start.39 = (bf16[3,64,128]{2,1,0:T(8,128)(2,1)}, bf16[3,64,128]{2,1,0:T(8,128)(2,1)S(1)}, u32[]{:S(2)}) copy-start(bf16[3,64,128]{2,1,0:T(8,128)(2,1)S(1)} %convolution_convert_fusion.13) | copy-start | bytes 147460
  19.1 54.6 %all-gather.10.cloned.1.call-start = ((), (), s32[]{:S(2)}) async-start(), calls=%async_computation.6 | async-start | bytes 1474560 | tf_op jit(solution)/shard_map/all_gather | solution.py:148
  19.8 73.1 %all-gather.8.cloned.1.call-start = ((), (), s32[]{:S(2)}) async-start(), calls=%async_computation.5 | async-start | bytes 1474560 | tf_op jit(solution)/shard_map/all_gather | solution.py:149
  20.6 99.8 %reduce-scatter.5.cloned.1.call-start = ((), (), s32[]{:S(2)}) async-start(), calls=%async_computation.7 | async-start | bytes 245760 | tf_op jit(solution)/shard_map/reduce_scatter | solution.py:174
  55.7 21.3 %copy-start.60 = (f32[128]{0:T(128)}, f32[128]{0:T(128)S(1)}, u32[]{:S(2)}) copy-start(f32[128]{0:T(128)S(1)} %fusion.97) | copy-start | bytes 1540
  61.8 15.2 %copy-start.18 = (bf16[128,768]{0,1:T(8,128)(2,1)}, bf16[128,768]{0,1:T(8,128)(2,1)S(1)}, u32[]{:S(2)}) copy-start(bf16[128,768]{0,1:T(8,128)(2,1)S(1)} %all_gather.19) | copy-start | bytes 589828
  78.5 6.6 copy-start.1
  97.9 22.5 %copy-start.24 = (bf16[192,768]{1,0:T(8,128)(2,1)S(1)}, bf16[192,768]{1,0:T(8,128)(2,1)}, u32[]{:S(2)}) copy-start(bf16[192,768]{1,0:T(8,128)(2,1)} %param.39) | copy-start | bytes 884740
  100.4 54.5 %all-reduce.12.cloned.1.call-start = ((), (), s32[]{:S(2)}) async-start(), calls=%async_computation.8 | async-start | bytes 393216 | tf_op jit(solution)/shard_map/psum | solution.py:178
  122.1 72.9 %all-reduce.14.cloned.1.call-start = ((), (), s32[]{:S(2)}) async-start(), calls=%async_computation.9 | async-start | bytes 393216 | tf_op jit(solution)/shard_map/psum | solution.py:203
  163.1 51.0 %all-gather.12.cloned.1.call-start = ((), (), s32[]{:S(2)}) async-start(), calls=%async_computation.10 | async-start | bytes 1474560 | tf_op jit(solution)/shard_map/all_gather | solution.py:151
  163.9 104.9 %reduce-scatter.7.cloned.1.call-start = ((), (), s32[]{:S(2)}) async-start(), calls=%async_computation.11 | async-start | bytes 245760 | tf_op jit(solution)/shard_map/reduce_scatter | solution.py:256
  235.7 9.8 %copy-start.7 = (bf16[1536,768]{0,1:T(8,128)(2,1)S(1)}, bf16[1536,768]{0,1:T(8,128)(2,1)}, u32[]{:S(2)}) copy-start(bf16[1536,768]{0,1:T(8,128)(2,1)} %copy-done.6) | copy-start | bytes 7077892
  247.9 55.7 %all-reduce.16.cloned.1.call-start = ((), (), s32[]{:S(2)}) async-start(), calls=%async_computation.12 | async-start | bytes 393216 | tf_op jit(solution)/shard_map/psum | solution.py:270
  270.7 61.0 %reduce-scatter.9.cloned.1.call-start = ((), (), s32[]{:S(2)}) async-start(), calls=%async_computation.13 | async-start | bytes 1474560 | tf_op jit(solution)/shard_map/reduce_scatter | solution.py:259
  275.5 84.8 %reduce-scatter.11.cloned.1.call-start = ((), (), s32[]{:S(2)}) async-start(), calls=%async_computation.14 | async-start | bytes 1474560 | tf_op jit(solution)/shard_map/reduce_scatter | solution.py:262
  294.4 13.5 %copy-start.55 = (f32[3,128]{1,0:T(4,128)S(1)}, f32[3,128]{1,0:T(4,128)}, u32[]{:S(2)}) copy-start(f32[3,128]{1,0:T(4,128)} %copy-done.54) | copy-start | bytes 4612
  294.5 101.3 %all-reduce.20.cloned.1.call-start = ((), (), s32[]{:S(2)}) async-start(), calls=%async_computation.16 | async-start | bytes 786432 | tf_op jit(solution)/shard_map/psum | solution.py:185
  314.8 396.2 %all-reduce.18.cloned.1.call-start = ((), (), s32[]{:S(2)}) async-start(), calls=%async_computation.15 | async-start | bytes 18874368 | tf_op jit(solution)/shard_map/psum | solution.py:308
  366.8 29.0 %copy-start.59 = (f32[128]{0:T(128)S(1)}, f32[128]{0:T(128)}, u32[]{:S(2)}) copy-start(f32[128]{0:T(128)} %copy-done.57) | copy-start | bytes 1540
  366.8 30.1 %copy-start.56 = (f32[768]{0:T(1024)S(1)}, f32[768]{0:T(1024)}, u32[]{:S(2)}) copy-start(f32[768]{0:T(1024)} %get-tuple-element.163) | copy-start | bytes 9220
  (48 other events, 159.1 us)
Sparse Core Ops, SparseCore 0:
  19.2 35.2 all-reduce.9
  56.2 17.4 all-gather.9
  75.3 17.6 all-gather.7
  100.6 19.7 reduce-scatter.4
  123.2 31.7 all-reduce.11
  163.3 31.6 all-reduce.13
  196.6 17.4 all-gather.11
  248.0 20.7 reduce-scatter.6
  271.8 31.6 all-reduce.15
  306.0 25.7 reduce-scatter.8
  334.5 25.7 reduce-scatter.10
  363.1 32.7 all-reduce.19
  405.1 305.8 all-reduce.17
where the time goes:
time: 732 us; the launch traced here: 731 us
  waiting for transfers between devices  511 us (70%)
  matrix products  88.8 us (12%)
  blocking collectives  61.5 us (8%)
  other arithmetic  30.2 us (4%)
  local copies, waits for them, and re-layouts  22.4 us (3%)
  between operations  15.4 us (2%)
    psum x1, waiting for transfers between devices, shards(): lax.psum((grad_gain_self, grad_gain_cross, grad_gain_ffn, grad_query_self...  273 us
    psum x1, blocking collectives, shards(): lax.psum((grad_gain_self, grad_gain_cross, grad_gain_ffn, grad_query_self...  38.7 us
    psum x1, waiting for transfers between devices, shards(): after_self = flat_in + lax.psum(matmul(self_flat, output_self), 'tensor')  33.9 us
    psum x1, waiting for transfers between devices, shards(): lax.psum(matmul(cross_flat, output_cross).astype(jnp.bfloat16), 'tensor')  32.6 us
    psum x1, waiting for transfers between devices, shards(): lax.psum((matmul_right_t(gate_low, gate_weight) + matmul_right_t(up_low,...  31 us
    reduce_scatter x1, waiting for transfers between devices, shards(): lax.psum_scatter(value_part.astype(jnp.bfloat16), 'tensor', scatter_dimen...  26.7 us
    psum x1, waiting for transfers between devices, shards(): lax.psum(matmul(hidden_low, down_weight).astype(jnp.bfloat16), 'tensor')  23.4 us
    reduce_scatter x1, waiting for transfers between devices, shards(): lax.psum_scatter(partial_mix.astype(jnp.bfloat16), 'tensor', scatter_dime...  19.8 us
  transfers between devices with their start and end apart: 13, of which 13 were waited for; matrix products, arithmetic and copies ran while one was open for 9% of the time, Pallas kernels for 0%

commit v1 on v0

v1 whole, which is shorter than its diff:
```python
import functools

import jax
import jax.numpy as jnp
from jax import lax
from jax.experimental import pallas as pl
from jax.experimental.pallas import tpu as pltpu
from jax.sharding import PartitionSpec as P

DH = 64
EPS = 1e-06
NEG = -1000000000.0
HIGH = lax.Precision.HIGHEST
MESH = pl.DeviceIdType.MESH
BF = jnp.bfloat16
F32 = jnp.float32
VMEM = pl.BlockSpec(memory_space=pltpu.VMEM)


def rms_norm(values, gain):
    return values * lax.rsqrt(jnp.mean(values * values, axis=-1, keepdims=True) + EPS) * gain


def gated(gate_value, up_value):
    return jax.nn.gelu(gate_value, approximate=True) * up_value


def mm(left, right, dims):
    return lax.dot_general(left, right, ((dims[0], dims[1]), ((), ())), preferred_element_type=F32)


def matmul(left, right):
    return mm(left, right, ((1,), (0,)))


def matmul_left_t(left, right):
    return mm(left, right, ((0,), (0,)))


def matmul_right_t(left, right):
    return mm(left, right, ((1,), (1,)))


def remote(src, dst, send, recv, device):
    return pltpu.make_async_remote_copy(
        src_ref=src, dst_ref=dst, send_sem=send, recv_sem=recv, device_id=device, device_id_type=MESH
    )


def greet(devices):
    barrier = pltpu.get_barrier_semaphore()
    for device in devices:
        pl.semaphore_signal(barrier, inc=1, device_id=device, device_id_type=MESH)
    pl.semaphore_wait(barrier, len(devices))


def tensor_place():
    dp, me = lax.axis_index("dp"), lax.axis_index("tensor")
    core = lax.rem(me, 2)
    return dp, me, core, me // 2


def rows_at(start, size, step):
    return pl.ds(pl.multiple_of(start, step), size)


def tensor_sum_kernel(count, *refs):
    xs, outs = refs[:count], refs[count : 2 * count]
    near, half, far, send, recv = refs[2 * count :]
    dp, me, core, side = tensor_place()
    mate, across = (dp, side * 2 + 1 - core), (dp, (1 - side) * 2 + core)
    greet([mate, across])
    size = xs[0].shape[0] // 2
    mine, other = rows_at(core * size, size, size), rows_at((1 - core) * size, size, size)
    first = [remote(xs[a].at[other], near.at[a], send.at[0, a], recv.at[0, a], mate) for a in range(count)]
    second = [remote(half.at[a], far.at[a], send.at[1, a], recv.at[1, a], across) for a in range(count)]
    third = [remote(outs[a].at[mine], outs[a].at[mine], send.at[2, a], recv.at[2, a], mate) for a in range(count)]
    for copy in first:
        copy.start()
    for a in range(count):
        first[a].wait()
        half[a] = (xs[a][mine].astype(F32) + near[a].astype(F32)).astype(BF)
        second[a].start()
    for a in range(count):
        second[a].wait()
        outs[a][mine] = (half[a].astype(F32) + far[a].astype(F32)).astype(BF)
        third[a].start()
    for copy in third:
        copy.wait()


def tensor_sum(values, collective_id):
    count = len(values)
    rows, width = values[0].shape
    return pl.pallas_call(
        functools.partial(tensor_sum_kernel, count),
        out_shape=[jax.ShapeDtypeStruct((rows, width), BF)] * count,
        in_specs=[VMEM] * count,
        out_specs=[VMEM] * count,
        scratch_shapes=[
            pltpu.VMEM((count, rows // 2, width), BF),
            pltpu.VMEM((count, rows // 2, width), BF),
            pltpu.VMEM((count, rows // 2, width), BF),
            pltpu.SemaphoreType.DMA((3, count)),
            pltpu.SemaphoreType.DMA((3, count)),
        ],
        compiler_params=pltpu.CompilerParams(collective_id=collective_id, has_side_effects=True),
    )(*values)


def tensor_gather_kernel(count, *refs):
    xs, outs = refs[:count], refs[count : 2 * count]
    send, recv, local = refs[2 * count :]
    dp, me, core, side = tensor_place()
    mate, across = (dp, side * 2 + 1 - core), (dp, (1 - side) * 2 + core)
    greet([mate, across])
    size = xs[0].shape[0]
    mine, theirs = rows_at(me * size, size, size), rows_at(((1 - side) * 2 + core) * size, size, size)
    keep = [pltpu.make_async_copy(xs[a], outs[a].at[mine], local.at[a]) for a in range(count)]
    to_across = [remote(xs[a], outs[a].at[mine], send.at[0, a], recv.at[0, a], across) for a in range(count)]
    to_mate = [remote(xs[a], outs[a].at[mine], send.at[1, a], recv.at[1, a], mate) for a in range(count)]
    onward = [remote(outs[a].at[theirs], outs[a].at[theirs], send.at[2, a], recv.at[2, a], mate) for a in range(count)]
    for a in range(count):
        to_across[a].start()
    for a in range(count):
        to_mate[a].start()
        keep[a].start()
    for a in range(count):
        to_across[a].wait()
        onward[a].start()
    for a in range(count):
        to_mate[a].wait()
        keep[a].wait()
        onward[a].wait()


def tensor_gather(values, collective_id):
    count = len(values)
    rows, width = values[0].shape
    return pl.pallas_call(
        functools.partial(tensor_gather_kernel, count),
        out_shape=[jax.ShapeDtypeStruct((4 * rows, width), BF)] * count,
        in_specs=[VMEM] * count,
        out_specs=[VMEM] * count,
        scratch_shapes=[
            pltpu.SemaphoreType.DMA((3, count)),
            pltpu.SemaphoreType.DMA((3, count)),
            pltpu.SemaphoreType.DMA((count,)),
        ],
        compiler_params=pltpu.CompilerParams(collective_id=collective_id, has_side_effects=True),
    )(*values)


def mixture_kernel(parts, mix_ref, stat_ref, out_ref, total_ref, mixes, stats, send, recv):
    dp, me, core, side = tensor_place()
    peers = [lax.rem(me + k, parts) for k in range(1, parts)]
    greet([(dp, peer) for peer in peers])
    size = mix_ref.shape[0] // parts
    heads = size // DH
    first, second = [], []
    for k, peer in enumerate(peers):
        block = rows_at(peer * size, size, size)
        first.append(remote(mix_ref.at[block], mixes.at[k], send.at[0, k], recv.at[0, k], (dp, peer)))
        first.append(remote(stat_ref.at[peer], stats.at[k], send.at[1, k], recv.at[1, k], (dp, peer)))
    mine = rows_at(me * size, size, size)
    for k, peer in enumerate(peers):
        second.append(remote(out_ref.at[mine], out_ref.at[mine], send.at[2, k], recv.at[2, k], (dp, peer)))
        second.append(remote(total_ref.at[me], total_ref.at[me], send.at[3, k], recv.at[3, k], (dp, peer)))
    for copy in first:
        copy.start()
    for copy in first:
        copy.wait()
    own = stat_ref[me]
    others = [stats[k] for k in range(parts - 1)]
    everyone = [own] + others
    top = everyone[0]
    for stat in everyone[1:]:
        top = jnp.maximum(top, stat)
    scales = [jnp.exp(stat - top) for stat in everyone]
    denominator = scales[0]
    for scale in scales[1:]:
        denominator = denominator + scale
    total_ref[me] = top + jnp.log(denominator)
    shares = [scale / denominator for scale in scales]
    own_mix = mix_ref[mine].astype(F32)
    for h in range(heads):
        rows = slice(h * DH, (h + 1) * DH)
        sum_up = own_mix[rows] * shares[0][h : h + 1]
        for k in range(parts - 1):
            sum_up = sum_up + mixes[k, rows].astype(F32) * shares[k + 1][h : h + 1]
        out_ref[rows_at(me * size + h * DH, DH, DH)] = sum_up.astype(BF)
    for copy in second:
        copy.start()
    for copy in second:
        copy.wait()


def combine_mixture(mix, stat, collective_id):
    parts = stat.shape[0]
    rows, width = mix.shape
    return pl.pallas_call(
        functools.partial(mixture_kernel, parts),
        out_shape=[jax.ShapeDtypeStruct(mix.shape, BF), jax.ShapeDtypeStruct(stat.shape, F32)],
        in_specs=[VMEM] * 2,
        out_specs=[VMEM] * 2,
        scratch_shapes=[
            pltpu.VMEM((parts - 1, rows // parts, width), BF),
            pltpu.VMEM((parts - 1,) + stat.shape[1:], F32),
            pltpu.SemaphoreType.DMA((4, parts - 1)),
            pltpu.SemaphoreType.DMA((4, parts - 1)),
        ],
        compiler_params=pltpu.CompilerParams(collective_id=collective_id, has_side_effects=True),
    )(mix, stat)


def scatter_kernel(count, parts, *refs):
    xs, outs = refs[:count], refs[count : 2 * count]
    bufs, send, recv = refs[2 * count :]
    dp, me, core, side = tensor_place()
    peers = [lax.rem(me + k, parts) for k in range(1, parts)]
    greet([(dp, peer) for peer in peers])
    size = xs[0].shape[0] // parts
    copies = []
    for a in range(count):
        for k, peer in enumerate(peers):
            block = rows_at(peer * size, size, size)
            copies.append(remote(xs[a].at[block], bufs.at[a, k], send.at[a, k], recv.at[a, k], (dp, peer)))
    for copy in copies:
        copy.start()
    for copy in copies:
        copy.wait()
    for a in range(count):
        sum_up = xs[a][rows_at(me * size, size, size)].astype(F32)
        for k in range(parts - 1):
            sum_up = sum_up + bufs[a, k].astype(F32)
        outs[a][...] = sum_up


def tensor_scatter(values, parts, collective_id):
    count = len(values)
    rows, width = values[0].shape
    return pl.pallas_call(
        functools.partial(scatter_kernel, count, parts),
        out_shape=[jax.ShapeDtypeStruct((rows // parts, width), F32)] * count,
        in_specs=[VMEM] * count,
        out_specs=[VMEM] * count,
        scratch_shapes=[
            pltpu.VMEM((count, parts - 1, rows // parts, width), BF),
            pltpu.SemaphoreType.DMA((count, parts - 1)),
            pltpu.SemaphoreType.DMA((count, parts - 1)),
        ],
        compiler_params=pltpu.CompilerParams(collective_id=collective_id, has_side_effects=True),
    )(*values)


def dp_sum_kernel(ranks, chunks, x_ref, out_ref, near, half, far, *sems):
    near_send, near_recv, far_send, far_recv, back_send, back_recv, end_send, end_recv = sems
    dp, tensor = lax.axis_index("dp"), lax.axis_index("tensor")
    x, z = lax.rem(dp, 2), dp // 2
    mate = (z * 2 + 1 - x, tensor)
    peers = [(lax.rem(z + k, ranks), k - 1) for k in range(1, ranks)]
    places = [(peer * 2 + x, tensor) for peer, k in peers]
    greet([mate] + places)
    rows = x_ref.shape[0]
    size = rows // 2 // chunks
    part = size // ranks
    def mine(c):
        return x * (rows // 2) + c * size
    def other(c):
        return (1 - x) * (rows // 2) + c * size
    first = [remote(x_ref.at[rows_at(other(c), size, size)], near.at[c], near_send.at[c], near_recv.at[c], mate) for c in range(chunks)]
    for copy in first:
        copy.start()
    second, third, fourth = [], [], []
    for c in range(chunks):
        second.append([remote(half.at[c, rows_at(peer * part, part, part)], far.at[c, k], far_send.at[c, k], far_recv.at[c, k], place) for (peer, k), place in zip(peers, places)])
        block = rows_at(mine(c) + z * part, part, part)
        third.append([remote(out_ref.at[block], out_ref.at[block], back_send.at[c, k], back_recv.at[c, k], place) for (peer, k), place in zip(peers, places)])
        block = rows_at(mine(c), size, size)
        fourth.append(remote(out_ref.at[block], out_ref.at[block], end_send.at[c], end_recv.at[c], mate))
    def one(c):
        first[c].wait()
        half[c] = (x_ref[rows_at(mine(c), size, size)].astype(F32) + near[c].astype(F32)).astype(BF)
        for copy in second[c]:
            copy.start()
    def two(c):
        for copy in second[c]:
            copy.wait()
        total = half[c, rows_at(z * part, part, part)].astype(F32)
        for k in range(ranks - 1):
            total = total + far[c, k].astype(F32)
        out_ref[rows_at(mine(c) + z * part, part, part)] = total.astype(BF)
        for copy in third[c]:
            copy.start()
    def three(c):
        for copy in third[c]:
            copy.wait()
        fourth[c].start()
    for c in range(chunks):
        one(c)
        if c >= 1:
            two(c - 1)
        if c >= 2:
            three(c - 2)
    two(chunks - 1)
    if chunks >= 2:
        three(chunks - 2)
    three(chunks - 1)
    for copy in fourth:
        copy.wait()


def dp_sum(packed, ranks, collective_id):
    rows, width = packed.shape
    z = ranks // 2
    chunks = 4 if z <= 4 else 1
    size = rows // 2 // chunks
    shapes = []
    for shape in ((chunks,), (chunks, z - 1), (chunks, z - 1), (chunks,)):
        shapes += [pltpu.SemaphoreType.DMA(shape)] * 2
    return pl.pallas_call(
        functools.partial(dp_sum_kernel, z, chunks),
        out_shape=jax.ShapeDtypeStruct(packed.shape, BF),
        in_specs=[VMEM],
        out_specs=VMEM,
        scratch_shapes=[
            pltpu.VMEM((chunks, size, width), BF),
            pltpu.VMEM((chunks, size, width), BF),
            pltpu.VMEM((chunks, z - 1, size // z, width), BF),
        ]
        + shapes,
        compiler_params=pltpu.CompilerParams(
            collective_id=collective_id, has_side_effects=True, vmem_limit_bytes=40 << 20
        ),
    )(packed)


def shards(
    tensor_size,
    dp_size,
    decoder_in,
    encoder_out,
    out_grad,
    group_ids,
    target_mask,
    bucket_ids,
    gain_self,
    gain_cross,
    gain_ffn,
    query_self,
    key_self,
    value_self,
    output_self,
    query_cross,
    key_cross,
    value_cross,
    output_cross,
    gate_weight,
    up_weight,
    down_weight,
    position_bias,
):
    query_count, target_len, width = decoder_in.shape
    assert query_count == 1
    heads = query_self.shape[1] // DH
    own = heads * DH
    all_heads = heads * tensor_size
    group_count, bucket_count, _ = position_bias.shape
    rows = encoder_out.shape[1]
    units = gate_weight.shape[1]

    key_t, value_t, query_t, output_all = tensor_gather(
        [key_cross.T, value_cross.T, query_cross.T, output_cross], 0
    )
    encoder = encoder_out[0]
    x = decoder_in[0].astype(F32)
    positions = jnp.arange(target_len)
    causal = positions[None, :] <= positions[:, None]
    diagonal = positions[None, :] == positions[:, None]
    allowed = causal & ((target_mask[0][None, :] == 1) | diagonal)
    group_hot = (group_ids[0] == jnp.arange(group_count)).astype(F32)
    bucket_hot = (jnp.arange(bucket_count)[:, None] == bucket_ids.reshape(-1)[None, :]).astype(F32)
    table = jnp.einsum("g,gkh->kh", group_hot, position_bias, precision=HIGH)
    spread = jnp.einsum("kp,kh->hp", bucket_hot, table, precision=HIGH)
    bias = jnp.where(allowed[None], spread.reshape(heads, target_len, target_len), NEG)
    self_in = rms_norm(x, gain_self).astype(BF)

    def to_heads(values, count):
        return values.reshape(values.shape[0], count, DH)

    q_self = to_heads(matmul(self_in, query_self).astype(BF), heads)
    k_self = to_heads(matmul(self_in, key_self).astype(BF), heads)
    v_self = to_heads(matmul(self_in, value_self).astype(BF), heads)
    scores = jnp.einsum("ihd,jhd->hij", q_self, k_self, preferred_element_type=F32) + bias
    p_self = jax.nn.softmax(scores, axis=-1)
    p_self_low = p_self.astype(BF)
    att_self = jnp.einsum("hij,jhd->ihd", p_self_low, v_self, preferred_element_type=F32).astype(BF)
    att_self = att_self.reshape(target_len, own)
    (self_out,) = tensor_sum([matmul(att_self, output_self).astype(BF)], 1)
    x2 = x + self_out.astype(F32)
    cross_in = rms_norm(x2, gain_cross).astype(BF)
    q_all = to_heads(matmul_right_t(cross_in, query_t).astype(BF), all_heads)
    k_all = to_heads(matmul_right_t(encoder, key_t).astype(BF), all_heads)
    v_all = to_heads(matmul_right_t(encoder, value_t).astype(BF), all_heads)
    cross_scores = jnp.einsum("ihd,jhd->hij", q_all, k_all, preferred_element_type=F32)
    top = jnp.max(cross_scores, axis=-1, keepdims=True)
    part_lse = top + jnp.log(jnp.sum(jnp.exp(cross_scores - top), axis=-1, keepdims=True))
    weights = jnp.exp(cross_scores - part_lse).astype(BF)
    part_mix = jnp.einsum("hij,jhd->hdi", weights, v_all, preferred_element_type=F32)
    stat = jnp.zeros((tensor_size, 8, target_len), F32)
    stat = stat.at[:, :heads].set(part_lse.reshape(tensor_size, heads, target_len))
    mix_t, total = combine_mixture(part_mix.astype(BF).reshape(all_heads * DH, target_len), stat, 2)
    lse = total[:, :heads].reshape(all_heads, target_len, 1)
    att_cross = mix_t.T
    x3 = x2 + matmul(att_cross, output_all)
    ffn_in = rms_norm(x3, gain_ffn).astype(BF)
    gate_value = matmul(ffn_in, gate_weight)
    up_value = matmul(ffn_in, up_weight)
    hidden = gated(gate_value, up_value).astype(BF)
    ffn_part = matmul(hidden, down_weight).astype(BF)
    out_low = out_grad[0]
    grad_down = matmul_left_t(hidden, out_low)
    d_hidden = matmul_right_t(out_low, down_weight).astype(BF)
    _, gated_pull = jax.vjp(gated, gate_value, up_value)
    d_gate, d_up = gated_pull(d_hidden.astype(F32))
    d_gate, d_up = d_gate.astype(BF), d_up.astype(BF)
    grad_gate = matmul_left_t(d_gate, ffn_in)
    grad_up = matmul_left_t(d_up, ffn_in)
    ffn_in_part = matmul_right_t(d_gate, gate_weight) + matmul_right_t(d_up, up_weight)
    ffn_in_grad, ffn_out = tensor_sum([ffn_in_part.astype(BF), ffn_part], 3)
    block_out = (x3 + ffn_out.astype(F32)).astype(BF)[None]
    _, ffn_pull = jax.vjp(rms_norm, x3, gain_ffn)
    ffn_norm_grad, grad_gain_ffn = ffn_pull(ffn_in_grad.astype(F32))
    g2 = out_low.astype(F32) + ffn_norm_grad
    g2_low = g2.astype(BF)
    me = lax.axis_index("tensor")
    att_own = lax.dynamic_slice(mix_t, (me * own, 0), (own, target_len))
    grad_output_cross = matmul(att_own, g2_low)
    d_att = to_heads(matmul_right_t(g2_low, output_all).astype(BF), all_heads)
    p_cross = jnp.exp(cross_scores - lse)
    dp_cross = jnp.einsum("ihd,jhd->hij", d_att, v_all, preferred_element_type=F32)
    delta = jnp.sum(d_att.astype(F32) * att_cross.reshape(target_len, all_heads, DH).astype(F32), axis=-1)
    ds_cross = (p_cross * (dp_cross - delta.T[:, :, None])).astype(BF)
    dk = jnp.einsum("hij,ihd->jhd", ds_cross, q_all, preferred_element_type=F32).astype(BF).reshape(rows, -1)
    dv = jnp.einsum("hij,ihd->jhd", p_cross.astype(BF), d_att, preferred_element_type=F32).astype(BF).reshape(rows, -1)
    dq_part = jnp.einsum("hij,jhd->ihd", ds_cross, k_all, preferred_element_type=F32).astype(BF)
    (dq,) = tensor_sum([dq_part.reshape(target_len, -1)], 4)
    encoder_grad = (matmul(dk, key_t) + matmul(dv, value_t)).astype(BF)[None]
    key_part = matmul_left_t(dk, encoder).astype(BF)
    value_part = matmul_left_t(dv, encoder).astype(BF)
    grad_key_cross, grad_value_cross = tensor_scatter([key_part, value_part], tensor_size, 5)
    dq_own = lax.dynamic_slice(dq, (0, me * own), (target_len, own))
    grad_query_cross = matmul_left_t(dq_own, cross_in)
    cross_in_grad = matmul(dq, query_t)
    _, cross_pull = jax.vjp(rms_norm, x2, gain_cross)
    cross_norm_grad, grad_gain_cross = cross_pull(cross_in_grad)
    g1 = g2 + cross_norm_grad
    g1_low = g1.astype(BF)
    grad_output_self = matmul_left_t(att_self, g1_low)
    d_att_self = to_heads(matmul_right_t(g1_low, output_self).astype(BF), heads)
    dp_self = jnp.einsum("ihd,jhd->hij", d_att_self, v_self, preferred_element_type=F32)
    inner = jnp.sum(p_self * dp_self, axis=-1, keepdims=True)
    ds_self = (p_self * (dp_self - inner)).astype(BF)
    sv = jnp.einsum("hij,ihd->jhd", p_self_low, d_att_self, preferred_element_type=F32).astype(BF).reshape(target_len, own)
    sk = jnp.einsum("hij,ihd->jhd", ds_self, q_self, preferred_element_type=F32).astype(BF).reshape(target_len, own)
    sq = jnp.einsum("hij,jhd->ihd", ds_self, k_self, preferred_element_type=F32).astype(BF).reshape(target_len, own)
    table_grad = jnp.einsum(
        "hp,kp->kh", ds_self.reshape(heads, -1), bucket_hot.astype(BF), preferred_element_type=F32
    )
    grad_position = group_hot[:, None, None] * table_grad[None]
    grad_query_self = matmul_left_t(sq, self_in)
    grad_key_self = matmul_left_t(sk, self_in)
    grad_value_self = matmul_left_t(sv, self_in)
    self_part = matmul_right_t(sq, query_self) + matmul_right_t(sk, key_self) + matmul_right_t(sv, value_self)
    (self_in_grad,) = tensor_sum([self_part.astype(BF)], 6)
    _, self_pull = jax.vjp(rms_norm, x, gain_self)
    self_norm_grad, grad_gain_self = self_pull(self_in_grad.astype(F32))
    decoder_grad = (g1 + self_norm_grad).astype(BF)[None]
    small = lax.psum((grad_gain_self, grad_gain_cross, grad_gain_ffn, grad_position), "dp")
    pieces = [
        grad_query_self, grad_key_self, grad_value_self, grad_output_self,
        grad_query_cross, grad_key_cross, grad_value_cross, grad_output_cross,
        grad_gate, grad_up, grad_down,
    ]
    packed = jnp.concatenate([piece.astype(BF) for piece in pieces], axis=0)
    packed = dp_sum(packed, dp_size, 7)
    outs, at = [], 0
    for k, piece in enumerate(pieces):
        value = packed[at : at + piece.shape[0]].astype(F32)
        at += piece.shape[0]
        outs.append(value if k in (3, 7, 10) else value.T)
    return (block_out, decoder_grad, encoder_grad) + tuple(small[:3]) + tuple(outs) + (small[3],)


def solution(mesh):
    rows = P("dp", None, None)
    encoder = P("dp", "tensor", None)
    columns, lines, whole = P(None, "tensor"), P("tensor", None), P()
    head_table = P(None, None, "tensor")
    weights = (columns, columns, columns, lines, columns, columns, columns, lines, columns, columns, lines, head_table)
    return jax.shard_map(
        functools.partial(shards, mesh.shape["tensor"], mesh.shape["dp"]),
        mesh=mesh,
        in_specs=(rows, encoder, rows, P("dp"), P("dp", None), whole, whole, whole, whole) + weights,
        out_specs=(rows, rows, encoder, whole, whole, whole) + weights,
        check_vma=False,
    )
```

time: 732 us -> 416 us (0.57)
  waiting for transfers between devices: 511 us -> 0 us
  Pallas kernels: 0 us -> 254 us
  blocking collectives: 61.5 us -> 38.6 us
  between operations: 15.4 us -> 2.32 us
  matrix products: 88.8 us -> 78.2 us
  other arithmetic: 30.2 us -> 22.6 us
    psum x6 -> x0, waiting for transfers between devices: 401 us -> none  [the longest x1 273 us: shards(): lax.psum((grad_gain_self, grad_gain_cross, grad_gain_ffn, grad_query_self...]
    pallas_call x0 -> x8, Pallas kernels: none -> 254 us  [the longest x1 142 us: dp_sum(): pl.pallas_call(functools.partial(dp_sum_kernel, z, chunks), out_shape=jax...]
    reduce_scatter x4 -> x0, waiting for transfers between devices: 79.7 us -> none  [the longest x1 26.7 us: shards(): lax.psum_scatter(value_part.astype(jnp.bfloat16), 'tensor', scatter_dimen...]
    all_gather x3 -> x0, waiting for transfers between devices: 28.9 us -> none  [the longest x1 14.9 us: shards(): lax.all_gather(output_cross, 'tensor', axis=0, tiled=True)]
    all_gather x3 -> x0, blocking collectives: 16.1 us -> none  [the longest x2 10.5 us: merged(): everything = jax.tree.map(lambda part: lax.all_gather(part, axis), shard)]
    dot_general x48, matrix products: 88.8 us -> 78.2 us  [the longest x33 55.2 us: mm(): lax.dot_general(left, right, ((dims[0], dims[1]), ((), ())), preferred_el...]
    psum x2 -> x1, blocking collectives: 45.4 us -> 38.6 us  [shards(): lax.psum((grad_gain_self, grad_gain_cross, grad_gain_ffn, grad_position),...]
    unnamed x146 -> x135, local copies, waits for them, and re-layouts: 19.6 us -> 13.5 us
  transfers between devices with their start and end apart: 13 -> 0, of which waited for: 13 -> 0; matrix products, arithmetic and copies ran while one was open for 9% -> 0% of each run, Pallas kernels for 0% -> 0%
where the time goes in v1:
time: 416 us; the launch traced here: 414 us
  Pallas kernels  254 us (61%)
  matrix products  78.2 us (19%)
  blocking collectives  38.6 us (9%)
  other arithmetic  22.6 us (5%)
  local copies, waits for them, and re-layouts  17.8 us (4%)
    pallas_call x1, Pallas kernels, dp_sum(): pl.pallas_call(functools.partial(dp_sum_kernel, z, chunks), out_shape=jax...  142 us
    dot_general x33, matrix products, mm(): lax.dot_general(left, right, ((dims[0], dims[1]), ((), ())), preferred_el...  55.2 us
    psum x1, blocking collectives, shards(): lax.psum((grad_gain_self, grad_gain_cross, grad_gain_ffn, grad_position),...  38.6 us
    pallas_call x4, Pallas kernels, tensor_sum(): pl.pallas_call(functools.partial(tensor_sum_kernel, count), out_shape=[ja...  38.2 us
    pallas_call x1, Pallas kernels, tensor_gather(): pl.pallas_call(functools.partial(tensor_gather_kernel, count), out_shape=...  34.7 us
    pallas_call x1, Pallas kernels, tensor_scatter(): pl.pallas_call(functools.partial(scatter_kernel, count, parts), out_shape...  29.7 us
    unnamed x135, local copies, waits for them, and re-layouts  13.5 us
    pallas_call x1, Pallas kernels, combine_mixture(): pl.pallas_call(functools.partial(mixture_kernel, parts), out_shape=[jax.S...  10.3 us

profile of v1, /device:TPU:0, one launch (start us, length us, event | category | flops | bytes accessed | tf_op | source)
XLA Modules:
  0.0 414.1 jit_solution(15127208594603711770)
XLA Ops:
  0.7 34.7 %shard_map.341 = (bf16[768,768]{1,0:T(8,128)(2,1)}, bf16[768,768]{1,0:T(8,128)(2,1)}, bf16[768,768]{1,0:T(8,128)(2,1)}, bf16[768,768]{1,0:T(8,128)(2,1)}) custom-call(bf16[192,768]{1,0:T(8,128)(2,1)} %bitcast.248, bf16[192,768]{1,0:T(8,128)(2,1)} %bitcast.249, bf16[192,768]{1,0:T(8,128)(2,1)} %bitcast.250, bf16[192,768]{1,0:T(8,128)(2,1)} %refs_3_.1), custom_call_target="tpu_custom_call" | custom-call | tf_op jit(solution)/shard_map/pallas_call | solution.py:140
  35.5 4.8 %convolution_convert_fusion.2 = bf16[768,1536]{1,0:T(8,128)(2,1)} fusion(bf16[768,768]{1,0:T(8,128)(2,1)} %get-tuple-element.40, bf16[1,1536,768]{2,1,0:T(8,128)(2,1)S(1)} %copy-done), kind=kOutput, calls=%fused_computation.14 | convolution fusion | flops 1813118976 | bytes 5898240 | tf_op jit(solution)/shard_map/dot_general | solution.py:29
  45.6 8.9 %shard_map.340 = bf16[128,768]{1,0:T(8,128)(2,1)} custom-call(bf16[128,768]{1,0:T(8,128)(2,1)} %convolution_convert_fusion.15.refs_0_), custom_call_target="tpu_custom_call" | custom-call | tf_op jit(solution)/shard_map/pallas_call | solution.py:95
  56.2 1.9 convolution_convert_fusion.14
  58.4 3.4 convolution_convert_fusion.1
  64.7 2.5 copy-done.1
  67.3 2.5 fusion.36
  70.4 10.3 %shard_map.342 = (bf16[768,128]{1,0:T(8,128)(2,1)}, f32[4,8,128]{2,1,0:T(8,128)}) custom-call(bf16[768,128]{1,0:T(8,128)(2,1)} %bitcast.245, f32[4,8,128]{2,1,0:T(8,128)} %scatter.4.stat_ref), custom_call_target="tpu_custom_call" | custom-call | tf_op jit(solution)/shard_map/pallas_call | solution.py:201
  80.7 1.9 multiply_reduce_fusion.3
  89.5 11.4 %shard_map.343 = (bf16[128,768]{1,0:T(8,128)(2,1)}, bf16[128,768]{1,0:T(8,128)(2,1)}) custom-call(bf16[128,768]{1,0:T(8,128)(2,1)} %fusion.34.refs_0_, bf16[128,768]{1,0:T(8,128)(2,1)} %convolution_convert_fusion.16.refs_1_), custom_call_target="tpu_custom_call" | custom-call | tf_op jit(solution)/shard_map/pallas_call | solution.py:95
  103.3 2.1 fusion.60
  107.9 6.8 %multiply_convert_fusion = bf16[12,128,1536]{2,1,0:T(8,128)(2,1)S(1)} fusion(f32[12,128,1536]{2,1,0:T(8,128)} %copy-done.1, bf16[128,12,64]{0,2,1:T(8,128)(2,1)S(1)} %bitcast.234, bf16[1536,12,64]{0,2,1:T(8,128)(2,1)} %bitcast.229, f32[12,128]{1,0:T(8,128)S(1)} %bitcast.264, f32[12,128]{1,0:T(8,128)S(1)} %sub.60), kind=kOutput, calls=%fused_computation.1 | convolution fusion | flops 311427072 | bytes 16723968 | tf_op jit(solution)/shard_map/ihd,jhd->hij/dot_general | solution.py:441
  117.8 8.9 %shard_map.344 = bf16[128,768]{1,0:T(8,128)(2,1)} custom-call(bf16[128,768]{1,0:T(8,128)(2,1)} %copy.55.refs_0_), custom_call_target="tpu_custom_call" | custom-call | tf_op jit(solution)/shard_map/pallas_call | solution.py:95
  126.8 2.4 multiply_reduce_fusion
  134.6 1.9 convolution_convert_fusion.18
  136.5 2.0 fusion.35.refs_0_
  138.5 8.9 %shard_map.345 = bf16[128,768]{1,0:T(8,128)(2,1)} custom-call(bf16[128,768]{1,0:T(8,128)(2,1)} %fusion.35.refs_0_), custom_call_target="tpu_custom_call" | custom-call | tf_op jit(solution)/shard_map/pallas_call | solution.py:95
  151.7 3.4 convolution_convert_fusion
  156.5 2.1 fusion.110
  158.6 2.1 fusion.7
  160.8 3.6 fusion.10
  167.4 38.6 %all-reduce.1 = (f32[768]{0:T(1024)}, f32[768]{0:T(1024)}, f32[768]{0:T(1024)}, f32[4,32,3]{1,0,2:T(4,128)}) all-reduce(f32[768]{0:T(1024)} %get-tuple-element.90, f32[768]{0:T(1024)} %get-tuple-element.86, f32[768]{0:T(1024)} %get-tuple-element.88, ...), channel_id=1, replica_groups=mesh['dp'=8,'tensor'=4] {'dp'}, use_global_device_ids=true, to_apply=%region_13.14 | all-reduce | flops 2688 | bytes 21504 | tf_op jit(solution)/shard_map/psum | solution.py:479
  213.2 1.9 fusion.28
  215.1 4.8 %fusion.18.refs_0_ = bf16[768,768]{1,0:T(8,128)(2,1)} fusion(bf16[1536,768]{0,1:T(8,128)(2,1)} %bitcast.237, bf16[1,1536,768]{2,1,0:T(8,128)(2,1)S(1)} %copy-done), kind=kOutput, calls=%fused_computation.27 | convolution fusion | flops 1812529152 | bytes 5898240 | tf_op jit(solution)/shard_map/dot_general | solution.py:29
  220.0 3.0 fusion.21.refs_1_
  223.0 29.7 %shard_map.346 = (f32[192,768]{1,0:T(8,128)}, f32[192,768]{1,0:T(8,128)}) custom-call(bf16[768,768]{1,0:T(8,128)(2,1)} %fusion.18.refs_0_, bf16[768,768]{1,0:T(8,128)(2,1)} %fusion.21.refs_1_), custom_call_target="tpu_custom_call" | custom-call | tf_op jit(solution)/shard_map/pallas_call | solution.py:242
  252.7 1.9 convert_dynamic-update-slice_fusion.1
  261.9 141.6 %shard_map.347 = bf16[3072,768]{1,0:T(8,128)(2,1)S(1)} custom-call(bf16[3072,768]{1,0:T(8,128)(2,1)} %fusion.24.x_ref), custom_call_target="tpu_custom_call" | custom-call | tf_op jit(solution)/shard_map/pallas_call | solution.py:321
  403.5 2.2 slice_convert_fusion.1
  405.7 2.3 slice_convert_fusion
  408.0 3.0 copy.60
  411.0 3.0 copy.61
  (199 shorter events, 53.1 us)
Async XLA Ops:
  0.7 34.8 %copy-start = (bf16[1,1536,768]{2,1,0:T(8,128)(2,1)S(1)}, bf16[1,1536,768]{2,1,0:T(8,128)(2,1)}, u32[]{:S(2)}) copy-start(bf16[1,1536,768]{2,1,0:T(8,128)(2,1)} %param.24) | copy-start | bytes 7077892
  35.4 4.9 %copy-start.3 = (bf16[1,128,768]{2,1,0:T(8,128)(2,1)S(1)}, bf16[1,128,768]{2,1,0:T(8,128)(2,1)}, u32[]{:S(2)}) copy-start(bf16[1,128,768]{2,1,0:T(8,128)(2,1)} %param.23) | copy-start | bytes 589828
  35.4 5.0 %copy-start.33 = (bf16[768,192]{0,1:T(8,128)(2,1)S(1)}, bf16[768,192]{0,1:T(8,128)(2,1)}, u32[]{:S(2)}) copy-start(bf16[768,192]{0,1:T(8,128)(2,1)} %param.34) | copy-start | bytes 884740
  35.4 5.0 %copy-start.44 = (f32[768]{0:T(1024)S(1)}, f32[768]{0:T(1024)}, u32[]{:S(2)}) copy-start(f32[768]{0:T(1024)} %param.29) | copy-start | bytes 9220
  35.5 5.4 %copy-start.34 = (bf16[768,192]{0,1:T(8,128)(2,1)S(1)}, bf16[768,192]{0,1:T(8,128)(2,1)}, u32[]{:S(2)}) copy-start(bf16[768,192]{0,1:T(8,128)(2,1)} %param.32) | copy-start | bytes 884740
  35.5 5.7 %copy-start.36 = (bf16[768,192]{0,1:T(8,128)(2,1)S(1)}, bf16[768,192]{0,1:T(8,128)(2,1)}, u32[]{:S(2)}) copy-start(bf16[768,192]{0,1:T(8,128)(2,1)} %param.33) | copy-start | bytes 884740
  35.5 6.7 %copy-start.51 = (f32[4,32,3]{1,0,2:T(4,128)S(1)}, f32[4,32,3]{1,0,2:T(4,128)}, u32[]{:S(2)}) copy-start(f32[4,32,3]{1,0,2:T(4,128)} %param.43) | copy-start | bytes 4612
  35.5 7.0 %copy-start.59 = (s32[128,128]{1,0:T(8,128)S(1)}, s32[128,128]{1,0:T(8,128)}, u32[]{:S(2)}) copy-start(s32[128,128]{1,0:T(8,128)} %param.28) | copy-start | bytes 196612
  41.1 13.4 %copy-start.40 = (bf16[128,192]{0,1:T(8,128)(2,1)}, bf16[128,192]{0,1:T(8,128)(2,1)S(1)}, u32[]{:S(2)}) copy-start(bf16[128,192]{0,1:T(8,128)(2,1)S(1)} %convolution_convert_fusion.24) | copy-start | bytes 147460
  41.5 16.7 %copy-start.42 = (bf16[128,192]{0,1:T(8,128)(2,1)}, bf16[128,192]{0,1:T(8,128)(2,1)S(1)}, u32[]{:S(2)}) copy-start(bf16[128,192]{0,1:T(8,128)(2,1)S(1)} %convolution_convert_fusion.23) | copy-start | bytes 147460
  41.5 14.7 %copy-start.47 = (f32[768]{0:T(1024)S(1)}, f32[768]{0:T(1024)}, u32[]{:S(2)}) copy-start(f32[768]{0:T(1024)} %param.30) | copy-start | bytes 9220
  43.7 14.6 %copy-start.24 = (f32[3,128,128]{1,2,0:T(8,128)}, f32[3,128,128]{1,2,0:T(8,128)S(1)}, u32[]{:S(2)}) copy-start(f32[3,128,128]{1,2,0:T(8,128)S(1)} %convolution_add_fusion.4) | copy-start | bytes 589828
  44.5 11.2 %copy-start.48 = (f32[3,128]{1,0:T(4,128)}, f32[3,128]{1,0:T(4,128)S(1)}, u32[]{:S(2)}) copy-start(f32[3,128]{1,0:T(4,128)S(1)} %get-tuple-element.112) | copy-start | bytes 4612
  44.7 11.0 %copy-start.38 = (bf16[3,64,128]{2,1,0:T(8,128)(2,1)}, bf16[3,64,128]{2,1,0:T(8,128)(2,1)S(1)}, u32[]{:S(2)}) copy-start(bf16[3,64,128]{2,1,0:T(8,128)(2,1)S(1)} %convolution_convert_fusion.21) | copy-start | bytes 147460
  56.2 5.5 %copy-start.52 = (f32[128]{0:T(128)}, f32[128]{0:T(128)S(1)}, u32[]{:S(2)}) copy-start(f32[128]{0:T(128)S(1)} %fusion.97) | copy-start | bytes 1540
  67.3 13.4 %copy-start.7 = (bf16[128,768]{1,0:T(8,128)(2,1)S(1)}, bf16[128,768]{1,0:T(8,128)(2,1)}, u32[]{:S(2)}) copy-start(bf16[128,768]{1,0:T(8,128)(2,1)} %shard_map.340) | copy-start | bytes 589828
  69.8 13.4 %copy-start.46 = (f32[768]{0:T(1024)S(1)}, f32[768]{0:T(1024)}, u32[]{:S(2)}) copy-start(f32[768]{0:T(1024)} %param.31) | copy-start | bytes 9220
  69.8 15.0 %copy-start.18 = (bf16[1,128,768]{2,1,0:T(8,128)(2,1)S(1)}, bf16[1,128,768]{2,1,0:T(8,128)(2,1)}, u32[]{:S(2)}) copy-start(bf16[1,128,768]{2,1,0:T(8,128)(2,1)} %param.25) | copy-start | bytes 589828
  80.7 5.6 %copy-start.23 = (bf16[768,512]{1,0:T(8,128)(2,1)S(1)}, bf16[768,512]{1,0:T(8,128)(2,1)}, u32[]{:S(2)}) copy-start(bf16[768,512]{1,0:T(8,128)(2,1)} %param.41) | copy-start | bytes 2359300
  106.1 8.6 %copy-start.9 = (bf16[128,768]{0,1:T(8,128)(2,1)}, bf16[128,768]{0,1:T(8,128)(2,1)S(1)}, u32[]{:S(2)}) copy-start(bf16[128,768]{0,1:T(8,128)(2,1)S(1)} %copy.54) | copy-start | bytes 589828
  107.9 6.8 %copy-start.6 = (bf16[768,1536]{1,0:T(8,128)(2,1)S(1)}, bf16[768,1536]{1,0:T(8,128)(2,1)}, u32[]{:S(2)}) copy-start(bf16[768,1536]{1,0:T(8,128)(2,1)} %copy-done.5) | copy-start | bytes 7077892
  117.0 12.2 %copy-start.55 = (f32[128]{0:T(128)S(1)}, f32[128]{0:T(128)}, u32[]{:S(2)}) copy-start(f32[128]{0:T(128)} %copy-done.54) | copy-start | bytes 1540
  126.8 4.9 %copy-start.43 = (bf16[128,192]{0,1:T(8,128)(2,1)S(1)}, bf16[128,192]{0,1:T(8,128)(2,1)}, u32[]{:S(2)}) copy-start(bf16[128,192]{0,1:T(8,128)(2,1)} %copy-done.42) | copy-start | bytes 147460
  149.9 6.6 %copy-start.58 = (bf16[768,768]{1,0:T(8,128)(2,1)S(1)}, bf16[768,768]{1,0:T(8,128)(2,1)}, u32[]{:S(2)}) copy-start(bf16[768,768]{1,0:T(8,128)(2,1)} %get-tuple-element.42) | copy-start | bytes 3538948
  151.7 6.9 %slice-start = ((s8[9437184]{0:T(1024)(128)(4,1)}), s8[4194304]{0:T(1024)(128)(4,1)S(1)}, s32[]{:S(2)}) async-start(s8[9437184]{0:T(1024)(128)(4,1)} %bitcast.227), calls=%async_computation | async-start | bytes 8388608
  151.7 6.9 %slice-start.1 = ((s8[9437184]{0:T(1024)(128)(4,1)}), s8[4194304]{0:T(1024)(128)(4,1)S(1)}, s32[]{:S(2)}) async-start(s8[9437184]{0:T(1024)(128)(4,1)} %bitcast.227), calls=%async_computation.1 | async-start | bytes 8388608
  215.1 4.8 %copy-start.17 = (bf16[12,64,1536]{2,1,0:T(8,128)(2,1)S(1)}, bf16[12,64,1536]{2,1,0:T(8,128)(2,1)}, u32[]{:S(2)}) copy-start(bf16[12,64,1536]{2,1,0:T(8,128)(2,1)} %copy-done.16) | copy-start | bytes 7077892
  223.0 35.1 %copy-start.14 = (bf16[128,768]{1,0:T(8,128)(2,1)S(1)}, bf16[128,768]{1,0:T(8,128)(2,1)}, u32[]{:S(2)}) copy-start(bf16[128,768]{1,0:T(8,128)(2,1)} %copy-done.13) | copy-start | bytes 589828
  223.0 35.1 %copy-start.31 = (bf16[128,512]{1,0:T(8,128)(2,1)S(1)}, bf16[128,512]{1,0:T(8,128)(2,1)}, u32[]{:S(2)}) copy-start(bf16[128,512]{1,0:T(8,128)(2,1)} %copy-done.30) | copy-start | bytes 393220
  252.6 6.7 %copy-start.29 = (bf16[128,512]{1,0:T(8,128)(2,1)S(1)}, bf16[128,512]{1,0:T(8,128)(2,1)}, u32[]{:S(2)}) copy-start(bf16[128,512]{1,0:T(8,128)(2,1)} %copy-done.28) | copy-start | bytes 393220
  252.7 8.0 %copy-start.19 = (bf16[1,128,768]{2,1,0:T(8,128)(2,1)S(1)}, bf16[1,128,768]{2,1,0:T(8,128)(2,1)}, u32[]{:S(2)}) copy-start(bf16[1,128,768]{2,1,0:T(8,128)(2,1)} %param.25) | copy-start | bytes 589828
  252.7 8.0 %copy-start.27 = (bf16[128,512]{1,0:T(8,128)(2,1)S(1)}, bf16[128,512]{1,0:T(8,128)(2,1)}, u32[]{:S(2)}) copy-start(bf16[128,512]{1,0:T(8,128)(2,1)} %copy-done.26) | copy-start | bytes 393220
  (34 other events, 89.2 us)

commit v2 on v0

v2 whole, which is shorter than its diff:
```python
import functools
from types import SimpleNamespace

import jax
import jax.numpy as jnp
from jax import lax
from jax.experimental import pallas as pl
from jax.experimental.pallas import tpu as pltpu
from jax.sharding import PartitionSpec as P

DH = 64
EPS = 1e-06
NEG = -1000000000.0
TILE = 256
MESH = pl.DeviceIdType.MESH
BF = jnp.bfloat16
F32 = jnp.float32
VMEM = pl.BlockSpec(memory_space=pltpu.VMEM)
SMEM = pl.BlockSpec(memory_space=pltpu.SMEM)
ANY = pl.BlockSpec(memory_space=pl.ANY)
GELU_SCALE = 0.7978845608028654
GELU_CUBIC = 0.044715


IN_X = (True, True, True, False, False, True, False, True, False, True, True, True, True, False)
SCHEDULE = (
    ((0, 0),),
    ((3, 0),),
    (),
    ((1, 0),),
    ((0, 1),),
    ((2, 0),),
    ((1, 1), (3, 1),),
    ((5, 0),),
    (),
    ((0, 2), (2, 1),),
    ((3, 2),),
    ((1, 2), (5, 1),),
    ((4, 0), (0, 3),),
    ((2, 2), (3, 3),),
    ((1, 3),),
    ((0, 4), (2, 3),),
    ((4, 1), (1, 4), (6, 0),),
    ((3, 4), (7, 0), (0, 5),),
    ((5, 2),),
    (),
    ((4, 2), (1, 5), (9, 0), (8, 0),),
    ((2, 4),),
    ((7, 1), (6, 1), (5, 3),),
    ((3, 5),),
    ((4, 3), (10, 0),),
    ((6, 2), (8, 1), (5, 4),),
    ((2, 5),),
    ((7, 2), (4, 4), (13, 0),),
    ((9, 1),),
    ((9, 2), (11, 0), (8, 2), (6, 3),),
    ((5, 5), (7, 3), (12, 0), (4, 5),),
    ((10, 1), (13, 1), (9, 3),),
    ((8, 3), (10, 2), (6, 4), (7, 4), (13, 2), (9, 4), (7, 5), (8, 4), (6, 5), (11, 1), (11, 2), (9, 5), (10, 3), (12, 1), (12, 2), (8, 5), (11, 3), (10, 4), (12, 3), (13, 3), (11, 4), (10, 5), (12, 4), (13, 4), (11, 5), (12, 5), (13, 5),),
)


def nn(left, right):
    return lax.dot_general(left, right, (((1,), (0,)), ((), ())), preferred_element_type=F32)


def nt(left, right):
    return lax.dot_general(left, right, (((1,), (1,)), ((), ())), preferred_element_type=F32)


def tn(left, right):
    return lax.dot_general(left, right, (((0,), (0,)), ((), ())), preferred_element_type=F32)


def span(start, size, step=None):
    return pl.ds(pl.multiple_of(start, step or size), size)


class Sems:
    def __init__(self, ref):
        self.ref, self.used = ref, 0

    def take(self):
        self.used += 1
        assert self.used <= self.ref.shape[0]
        return self.ref.at[self.used - 1]


class Wire:
    def __init__(self, sems, src, dst, device):
        self.copy = pltpu.make_async_remote_copy(
            src_ref=src, dst_ref=dst, send_sem=sems.take(), recv_sem=sems.take(), device_id=device, device_id_type=MESH
        )

    def start(self):
        self.copy.start()

    def sent(self):
        self.copy.wait_send()

    def came(self):
        self.copy.wait_recv()

    def wait(self):
        self.copy.wait()


class TensorSum:
    def __init__(self, sems, place, src, near, half, far, out):
        self.src, self.near, self.half, self.far, self.out = src, near, half, far, out
        size = src.shape[0] // 2
        self.mine = span(place.core * size, size)
        other = span((1 - place.core) * size, size)
        self.first = Wire(sems, src.at[other], near, place.mate)
        self.second = Wire(sems, half, far, place.across)
        self.third = Wire(sems, out.at[self.mine], out.at[self.mine], place.mate)

    def one(self):
        self.first.start()

    def two(self):
        self.first.wait()
        self.half[...] = (self.src[self.mine].astype(F32) + self.near[...].astype(F32)).astype(BF)
        self.second.start()

    def three(self):
        self.second.wait()
        self.out[self.mine] = (self.half[...].astype(F32) + self.far[...].astype(F32)).astype(BF)
        self.third.start()

    def four(self):
        self.third.wait()


class TensorMix:
    def __init__(self, sems, place, mix, stat, bufs, out, total):
        self.place, self.mix, self.stat, self.out, self.total = place, mix, stat, out, total
        near, half, far, near_stat, half_stat, far_stat = bufs
        self.bufs = bufs
        size, core = mix.shape[0] // 2, place.core
        self.size = size
        self.mine, other = span(core * size, size), span((1 - core) * size, size)
        self.mine_stat, other_stat = span(core * 8, 8), span((1 - core) * 8, 8)
        self.first = [
            Wire(sems, mix.at[other], near, place.mate),
            Wire(sems, stat.at[other_stat], near_stat, place.mate),
        ]
        self.second = [Wire(sems, half, far, place.across), Wire(sems, half_stat, far_stat, place.across)]
        self.third = [
            Wire(sems, out.at[self.mine], out.at[self.mine], place.mate),
            Wire(sems, total.at[self.mine_stat], total.at[self.mine_stat], place.mate),
        ]

    def join(self, ours, theirs, ours_stat, theirs_stat, flip, store):
        low_stat = jnp.where(flip, theirs_stat, ours_stat)
        high_stat = jnp.where(flip, ours_stat, theirs_stat)
        top = jnp.maximum(low_stat, high_stat)
        total = top + jnp.log(jnp.exp(low_stat - top) + jnp.exp(high_stat - top))
        low_share, high_share = jnp.exp(low_stat - total), jnp.exp(high_stat - total)
        for h in range(self.size // DH):
            rows = slice(h * DH, (h + 1) * DH)
            a, b = ours(rows), theirs(rows)
            low, high = jnp.where(flip, b, a), jnp.where(flip, a, b)
            store(rows, (low * low_share[h : h + 1] + high * high_share[h : h + 1]).astype(BF))
        return total

    def one(self):
        for wire in self.first:
            wire.start()

    def two(self):
        near, half, far, near_stat, half_stat, far_stat = self.bufs
        core, size = self.place.core, self.size
        for wire in self.first:
            wire.wait()

        def ours(rows):
            return self.mix[span(core * size + rows.start, DH)].astype(F32)

        def store(rows, value):
            half[rows] = value

        half_stat[...] = self.join(
            ours, lambda rows: near[rows].astype(F32), self.stat[self.mine_stat], near_stat[...], core == 1, store
        )
        for wire in self.second:
            wire.start()

    def three(self):
        near, half, far, near_stat, half_stat, far_stat = self.bufs
        core, size = self.place.core, self.size
        for wire in self.second:
            wire.wait()

        def store(rows, value):
            self.out[span(core * size + rows.start, DH)] = value

        self.total[self.mine_stat] = self.join(
            lambda rows: half[rows].astype(F32),
            lambda rows: far[rows].astype(F32),
            half_stat[...],
            far_stat[...],
            self.place.side == 1,
            store,
        )
        for wire in self.third:
            wire.start()

    def four(self):
        for wire in self.third:
            wire.wait()


class WeightGather:
    def __init__(self, sems, place, own, whole, local):
        rows = own.shape[0]
        half = rows // 2
        me, core, side, x = place.me, place.core, place.side, place.x
        there = (1 - side) * 2 + core
        self.own, self.whole = own, whole
        mine = span(me * rows, rows)
        direct = span(there * rows + x * half, half)
        relayed = span(there * rows + (1 - x) * half, half)
        self.across = Wire(sems, own.at[span(x * half, half)], whole.at[span(me * rows + x * half, half)], place.across)
        self.mate = Wire(sems, own, whole.at[mine], place.mate)
        self.side = Wire(sems, whole.at[direct], whole.at[direct], place.beside)
        self.direct = Wire(sems, whole.at[direct], whole.at[direct], place.mate)
        self.relayed = Wire(sems, whole.at[relayed], whole.at[relayed], place.mate)
        self.keep = pltpu.make_async_copy(own, whole.at[mine], local)

    def start(self):
        self.across.start()
        self.mate.start()
        self.keep.start()

    def one(self):
        self.across.came()
        self.side.start()
        self.direct.start()

    def two(self):
        self.side.came()
        self.relayed.start()

    def three(self):
        self.mate.came()
        self.keep.wait()
        self.direct.came()
        self.relayed.came()

    def end(self):
        for wire in (self.across, self.mate, self.side, self.direct, self.relayed):
            wire.sent()


class ChunkX:
    def __init__(self, sems, place, g, out, bufs):
        self.place = place
        near, inn, mid, tot, fin = self.bufs = bufs
        half = g.shape[0] // 2
        x = place.x
        self.g, self.mine = g, span(x * half, half)
        other = span((1 - x) * half, half)
        self.rs = Wire(sems, g.at[other], near, place.beside)
        self.out = Wire(sems, g.at[self.mine], inn, place.pair)
        self.middle = Wire(sems, g.at[self.mine], mid, place.middle)
        self.back = Wire(sems, tot, tot, place.pair)
        self.ag = Wire(sems, tot, fin, place.beside)
        self.save = [
            pltpu.make_async_copy(tot, out.at[self.mine], sems.take()),
            pltpu.make_async_copy(fin, out.at[other], sems.take()),
        ]

    def s0(self):
        self.rs.start()

    def s1(self):
        self.rs.wait()
        self.g[self.mine] = self.g[self.mine] + self.bufs[0][...]

        @pl.when(self.place.end)
        def _():
            self.out.start()

    def s2(self):
        @pl.when(self.place.inner)
        def _():
            self.out.came()
            self.g[self.mine] = self.g[self.mine] + self.bufs[1][...]
            self.middle.start()

    def s3(self):
        @pl.when(self.place.inner)
        def _():
            self.middle.wait()
            self.bufs[3][...] = self.g[self.mine] + self.bufs[2][...]
            self.back.start()
            self.ag.start()
            self.save[0].start()

    def s4(self):
        @pl.when(self.place.end)
        def _():
            self.back.came()
            self.ag.start()
            self.save[0].start()

    def s5(self):
        self.ag.came()
        self.save[1].start()

    def finish(self):
        @pl.when(self.place.end)
        def _():
            self.out.sent()

        @pl.when(self.place.inner)
        def _():
            self.back.sent()

        self.ag.sent()
        for copy in self.save:
            copy.wait()


class ChunkZ:
    def __init__(self, sems, place, g, out, bufs):
        self.place = place
        inn, mid, r, xr, tot = self.bufs = bufs
        half = g.shape[0] // 2
        at = place.high
        self.g, self.mine = g, span(at * half, half)
        self.other = span((1 - at) * half, half)
        self.out = Wire(sems, g, inn, place.pair)
        self.rs = Wire(sems, g.at[self.other], mid, place.middle)
        self.x = Wire(sems, r, xr, place.beside)
        self.ag = Wire(sems, tot.at[self.mine], tot.at[self.mine], place.middle)
        self.back = [
            Wire(sems, tot.at[self.mine], tot.at[self.mine], place.pair),
            Wire(sems, tot.at[self.other], tot.at[self.other], place.pair),
        ]
        self.save = pltpu.make_async_copy(tot, out, sems.take())

    def s0(self):
        @pl.when(self.place.end)
        def _():
            self.out.start()

    def s1(self):
        @pl.when(self.place.inner)
        def _():
            self.out.came()
            self.g[...] = self.g[...] + self.bufs[0][...]
            self.rs.start()

    def s2(self):
        @pl.when(self.place.inner)
        def _():
            self.rs.wait()
            self.bufs[2][...] = self.g[self.mine] + self.bufs[1][...]
            self.x.start()

    def s3(self):
        @pl.when(self.place.inner)
        def _():
            self.x.wait()
            self.bufs[4][self.mine] = self.bufs[2][...] + self.bufs[3][...]
            self.ag.start()
            self.back[0].start()

    def s4(self):
        @pl.when(self.place.inner)
        def _():
            self.ag.came()
            self.back[1].start()
            self.save.start()

    def s5(self):
        @pl.when(self.place.end)
        def _():
            for wire in self.back:
                wire.came()
            self.save.start()

    def finish(self):
        @pl.when(self.place.end)
        def _():
            self.out.sent()

        @pl.when(self.place.inner)
        def _():
            self.ag.sent()
            for wire in self.back:
                wire.sent()

        self.save.wait()


class SmallSum:
    def __init__(self, sems, place, bufs):
        self.place = place
        own, near, sum1, inn, sum2, mid, tot = self.bufs = bufs
        self.x = Wire(sems, own, near, place.beside)
        self.out = Wire(sems, sum1, inn, place.pair)
        self.middle = Wire(sems, sum2, mid, place.middle)
        self.back = Wire(sems, tot, tot, place.pair)

    def s0(self):
        self.x.start()

    def s1(self):
        own, near, sum1, inn, sum2, mid, tot = self.bufs
        self.x.wait()
        sum1[...] = own[...] + near[...]

        @pl.when(self.place.end)
        def _():
            self.out.start()

    def s2(self):
        own, near, sum1, inn, sum2, mid, tot = self.bufs

        @pl.when(self.place.inner)
        def _():
            self.out.came()
            sum2[...] = sum1[...] + inn[...]
            self.middle.start()

    def s3(self):
        own, near, sum1, inn, sum2, mid, tot = self.bufs

        @pl.when(self.place.inner)
        def _():
            self.middle.wait()
            tot[...] = sum2[...] + mid[...]
            self.back.start()
            self.back.sent()

    def s4(self):
        @pl.when(self.place.end)
        def _():
            self.out.sent()
            self.back.came()


def rms_scale(values):
    return lax.rsqrt(jnp.mean(values * values, axis=-1, keepdims=True) + EPS)


def norm_back(values, gain, dy):
    scale = rms_scale(values)
    normal = values * scale
    gain_grad = jnp.sum(dy * normal, axis=0, keepdims=True)
    pulled = dy * gain
    mean = jnp.mean(pulled * normal, axis=-1, keepdims=True)
    return scale * (pulled - normal * mean), gain_grad


def fold(values, op):
    rows, width = values.shape
    return op(values.reshape(rows // 8, 8, width), axis=0)


def chunk_plan(own, width, units):
    plan = [(0, k * (units // 2), units // 2) for k in range(2)]
    plan += [(a, k * (width // 2), width // 2) for a in (1, 2) for k in range(2)]
    plan += [(3, k * own, own) for k in range(8)]
    return [(in_x, *block) for in_x, block in zip(IN_X, plan)]


def block_kernel(cfg, *refs):
    groups, at = [], 0
    for tree in cfg.trees:
        groups.append(SimpleNamespace(**jax.tree.unflatten(tree, refs[at : at + tree.num_leaves])))
        at += tree.num_leaves
    ins, outs, scr = groups
    gain_self, gain_cross, gain_ffn = (gain[...].reshape(1, cfg.width) for gain in ins.gains)
    heads, all_heads, width, tokens, rows = cfg.heads, cfg.all_heads, cfg.width, cfg.tokens, cfg.rows
    own, pairs, tiles = heads * DH, all_heads // 2, rows // TILE
    summing = cfg.summing
    sems = Sems(scr.sems)
    dp, me = lax.axis_index("dp"), lax.axis_index("tensor")
    core, side = lax.rem(me, 2), me // 2
    x, z = lax.rem(dp, 2), dp // 2
    place = SimpleNamespace(
        me=me,
        core=core,
        side=side,
        x=x,
        mate=(dp, side * 2 + 1 - core),
        across=(dp, (1 - side) * 2 + core),
        beside=(dp + 1 - 2 * x, me),
    )
    barrier = pltpu.get_barrier_semaphore()
    for friend in (place.mate, place.across, place.beside):
        pl.semaphore_signal(barrier, inc=1, device_id=friend, device_id_type=MESH)
    if summing:
        inner = jnp.logical_or(z == 1, z == 2)
        place.inner, place.end = inner, jnp.logical_not(inner)
        place.high = z // 2
        place.pair = ((z + 1 - 2 * lax.rem(z, 2)) * 2 + x, me)
        place.middle = ((3 - z) * 2 + x, me)
        pl.semaphore_signal(barrier, inc=1, device_id=place.pair, device_id_type=MESH)

        @pl.when(inner)
        def _():
            pl.semaphore_signal(barrier, inc=1, device_id=place.middle, device_id_type=MESH)

    def fetch(src, dst):
        copy = pltpu.make_async_copy(src, dst, sems.take())
        copy.start()
        return copy

    enc, down, gate_w, up_w = scr.enc, scr.down, scr.gate_w, scr.up_w
    load_enc = fetch(ins.encoder, enc)
    load_ffn = [fetch(ins.down_w, down), fetch(ins.gate_w, gate_w), fetch(ins.up_w, up_w)]

    xv = ins.x[...].astype(F32)
    self_in = scr.self_in
    self_in[...] = (xv * rms_scale(xv) * gain_self).astype(BF)
    qkv = scr.qkv
    self_weights = (ins.wq_self, ins.wk_self, ins.wv_self)
    for k, weight in enumerate(self_weights):
        qkv[k * own : (k + 1) * own] = nt(weight[...], self_in[...]).astype(BF)
    if summing:
        pl.semaphore_wait(barrier, 4 + inner.astype(jnp.int32))
    else:
        pl.semaphore_wait(barrier, 3)
    wk, wq, wv, wo = scr.wk, scr.wq, scr.wv, scr.wo
    get_k, get_q, get_v, get_o = gathers = [
        WeightGather(sems, place, part, whole, sems.take())
        for part, whole in ((ins.wk_cross, wk), (ins.wq_cross, wq), (ins.wv_cross, wv), (ins.wo_cross, wo))
    ]
    get_k.start()
    get_q.start()
    scr.bucket[...] = ins.bucket[...].T
    bucket = scr.bucket
    keep = jnp.broadcast_to(ins.mask[...].astype(F32), (tokens, tokens)).T
    j_at = lax.broadcasted_iota(jnp.int32, (tokens, tokens), 0)
    i_at = lax.broadcasted_iota(jnp.int32, (tokens, tokens), 1)
    allowed = jnp.logical_or(jnp.logical_and(j_at <= i_at, keep == 1.0), j_at == i_at)
    group = ins.group[0]
    buckets = cfg.buckets
    for h in range(heads):
        scr.p_self[h] = jnp.full((tokens, tokens), NEG, F32)

    def spread(b, _):
        hit = jnp.logical_and(bucket[...] == b, allowed)
        for h in range(heads):
            scr.p_self[h] = jnp.where(hit, ins.table[h, group, b], scr.p_self[h])
        return 0

    lax.fori_loop(0, buckets, spread, 0)
    get_v.start()
    att_self = scr.att_self

    def attend(h):
        q = qkv[h * DH : (h + 1) * DH]
        k = qkv[own + h * DH : own + (h + 1) * DH]
        v = qkv[2 * own + h * DH : 2 * own + (h + 1) * DH]
        s = tn(k, q) + scr.p_self[h]
        e = jnp.exp(s - jnp.max(s, axis=0, keepdims=True))
        p = e / jnp.sum(e, axis=0, keepdims=True)
        scr.p_self[h] = p
        att_self[h * DH : (h + 1) * DH] = nn(v, p.astype(BF)).astype(BF)

    attend(0)
    get_o.start()
    for h in range(1, heads):
        attend(h)
    get_k.one()

    def tensor_sum(bufs):
        return TensorSum(sems, place, *bufs)

    s1 = tensor_sum(scr.s1)
    s1.src[...] = tn(att_self[...], ins.wo_self[...]).astype(BF)
    s1.one()
    get_q.one()
    get_k.two()
    s1.two()
    get_v.one()
    get_q.two()
    get_o.one()
    get_v.two()
    load_enc.wait()
    get_k.three()
    kc, vc, kt, vt, e_ref = scr.kc, scr.vc, scr.kt, scr.vt, scr.e

    def project(dst, weight):
        def body(r, _):
            at = span(r * TILE, TILE)
            dst[at] = nt(enc[at], weight[...]).astype(BF)
            return 0

        lax.fori_loop(0, tiles, body, 0)

    def project_t(dst, weight):
        def body(r, _):
            at = span(r * TILE, TILE)
            dst[:, at] = nt(weight[...], enc[at]).astype(BF)
            return 0

        lax.fori_loop(0, tiles, body, 0)

    project(kc, wk)
    s1.three()
    get_o.two()
    get_v.three()
    project_t(vt, wv)
    s1.four()
    x2 = scr.x2
    x2[...] = xv + s1.out[...].astype(F32)
    cross_in = scr.cross_in
    cross_in[...] = (x2[...] * rms_scale(x2[...]) * gain_cross).astype(BF)
    get_q.three()
    bq, bw = scr.bq, scr.bw
    bq[...] = jnp.zeros(bq.shape, BF)
    bw[...] = jnp.zeros(bw.shape, BF)
    q_t = nt(wq[...], cross_in[...]).astype(BF)
    for h in range(all_heads):
        at = slice(h * DH, (h + 1) * DH)
        bq[at, (h % 2) * tokens : (h % 2 + 1) * tokens] = q_t[at]
    s_ref, mix, stat, top_ref = scr.s, scr.mix, scr.stat, scr.top
    stat[...] = jnp.zeros(stat.shape, F32)
    top_ref[...] = jnp.zeros(top_ref.shape, F32)
    per_half = pairs // 2

    def stat_row(p):
        return (p // per_half) * 8 + 2 * (p - (p // per_half) * per_half)

    def forward_pair(p, _):
        head_at = span(p * 2 * DH, 2 * DH)
        score_at = span(p * 2 * tokens, 2 * tokens)
        weights = bq[head_at]
        top = None
        for r in range(tiles):
            at = slice(r * TILE, (r + 1) * TILE)
            s = nn(kc[at, head_at], weights)
            s_ref[at] = s
            part = fold(s, jnp.max)
            top = part if top is None else jnp.maximum(top, part)
        top = jnp.max(top, axis=0, keepdims=True)
        total, acc = None, None
        for r in range(tiles):
            at = slice(r * TILE, (r + 1) * TILE)
            e = jnp.exp(s_ref[at] - top)
            part = fold(e, jnp.sum)
            total = part if total is None else total + part
            low = e.astype(BF)
            e_ref[at, score_at] = low
            part = nn(vt[head_at, at], low)
            acc = part if acc is None else acc + part
        total = jnp.sum(total, axis=0, keepdims=True)
        inverse = 1.0 / total
        lse = top + jnp.log(total)
        row = stat_row(p)
        for k in range(2):
            lanes = slice(k * tokens, (k + 1) * tokens)
            value = acc[k * DH : (k + 1) * DH, lanes] * inverse[:, lanes]
            mix[span(p * 2 * DH + k * DH, DH)] = value.astype(BF)
            stat[pl.ds(row + k, 1)] = lse[:, lanes]
            top_ref[pl.ds(row + k, 1)] = top[:, lanes]
        return 0

    lax.fori_loop(0, pairs, forward_pair, 0)
    att, lse = scr.att, scr.lse
    s2 = TensorMix(sems, place, mix, stat, scr.mix_bufs, att, lse)
    s2.one()
    for load in load_ffn:
        load.wait()
    og = ins.out_grad
    scr.d_hidden[...] = nt(og[...], down[...]).astype(BF).astype(F32)
    s2.two()
    project(vc, wv)
    s2.three()
    get_o.three()
    s2.four()
    x3 = scr.x3
    x3[...] = x2[...] + tn(att[...], wo[...])
    ffn_in = scr.ffn_in
    ffn_in[...] = (x3[...] * rms_scale(x3[...]) * gain_ffn).astype(BF)
    gate = nn(ffn_in[...], gate_w[...])
    up = nn(ffn_in[...], up_w[...])
    squared = gate * gate
    curve = jnp.tanh(GELU_SCALE * (gate + GELU_CUBIC * (squared * gate)))
    gelu = 0.5 * gate * (1.0 + curve)
    slope = 0.5 * (1.0 + curve) + 0.5 * gate * (1.0 - curve * curve) * (
        GELU_SCALE * (1.0 + 3.0 * GELU_CUBIC * squared)
    )
    d_hidden = scr.d_hidden[...]
    scr.hidden[...] = (gelu * up).astype(BF)
    scr.d_gate[...] = (d_hidden * up * slope).astype(BF)
    scr.d_up[...] = (d_hidden * gelu).astype(BF)

    chunks = []
    if summing:
        for (in_x, source, start, size), bufs in zip(cfg.chunks, scr.chunks):
            rows_at = pl.ds(start, size)
            maker = ChunkX if in_x else ChunkZ
            chunks.append(maker(sems, place, scr.grads[source].at[rows_at], outs.grads[source].at[rows_at], bufs))
    schedule = iter(cfg.schedule)

    def poll():
        if summing:
            for n, k in next(schedule):
                chunk = chunks[n]
                (chunk.s0, chunk.s1, chunk.s2, chunk.s3, chunk.s4, chunk.s5)[k]()

    g_down, g_gate, g_up, g_small = scr.grads
    g_down[...] = tn(scr.hidden[...], og[...]).astype(BF)
    poll()
    g_gate[...] = tn(ffn_in[...], scr.d_gate[...]).astype(BF)
    poll()
    g_up[...] = tn(ffn_in[...], scr.d_up[...]).astype(BF)
    poll()
    s3, so = tensor_sum(scr.s3), tensor_sum(scr.so)
    s3.src[...] = (nt(scr.d_gate[...], gate_w[...]) + nt(scr.d_up[...], up_w[...])).astype(BF)
    s3.one()
    so.src[...] = nn(scr.hidden[...], down[...]).astype(BF)
    s3.two()
    poll()
    project_t(kt, wk)
    poll()
    s3.three()
    so.one()
    s3.four()
    so.two()
    poll()
    g2, g2_low = scr.g2, scr.g2_low
    dv, gain_grad = norm_back(x3[...], gain_ffn, s3.out[...].astype(F32))
    g2[...] = og[...].astype(F32) + dv
    g2_low[...] = g2[...].astype(BF)
    small = scr.small[0]
    small[...] = jnp.zeros(small.shape, F32)
    small[2:3, :width] = gain_grad
    g_small[0:own] = nn(att[span(me * own, own)], g2_low[...]).astype(BF)
    poll()
    d_att = nt(wo[...], g2_low[...])
    delta_ref = scr.delta
    for h in range(all_heads):
        at = slice(h * DH, (h + 1) * DH)
        p, k = divmod(h, 2)
        row = (p // per_half) * 8 + 2 * (p % per_half) + k
        share = jnp.exp(top_ref[row : row + 1] - lse[row : row + 1])
        low = (d_att[at] * share).astype(BF)
        bw[at, k * tokens : (k + 1) * tokens] = low
        delta_ref[p : p + 1, k * tokens : (k + 1) * tokens] = jnp.sum(
            low.astype(F32) * att[at].astype(F32), axis=0, keepdims=True
        )
    so.three()
    s4 = tensor_sum(scr.s4)

    def backward_pair(p, _):
        head_at = span(p * 2 * DH, 2 * DH)
        score_at = span(p * 2 * tokens, 2 * tokens)
        wq_block, wa_block = bq[head_at], bw[head_at]
        delta = delta_ref[pl.ds(p, 1)]
        acc = None
        for r in range(tiles):
            at = slice(r * TILE, (r + 1) * TILE)
            e = e_ref[at, score_at]
            grad = nn(vc[at, head_at], wa_block)
            ds = (e.astype(F32) * (grad - delta)).astype(BF)
            part = nn(kt[head_at, at], ds)
            acc = part if acc is None else acc + part
            kc[at, head_at] = nt(ds, wq_block).astype(BF)
            vc[at, head_at] = nt(e, wa_block).astype(BF)
            kt[head_at, at] = nt(wq_block, ds).astype(BF)
            vt[head_at, at] = nt(wa_block, e).astype(BF)
        for k in range(2):
            value = acc[k * DH : (k + 1) * DH, k * tokens : (k + 1) * tokens]
            s4.src[span(p * 2 * DH + k * DH, DH)] = value.astype(BF)
        return 0

    for p in range(pairs):
        poll()
        lax.fori_loop(p, p + 1, backward_pair, 0)
    s4.one()
    so.four()
    outs.block_out[...] = (x3[...] + so.out[...].astype(F32)).astype(BF)
    poll()

    parts, kv_near, kv_half, kv_far = scr.parts, scr.kv_near, scr.kv_half, scr.kv_far
    to_mate, to_across = [], []
    for a in range(2):
        to_mate.append(
            Wire(sems, parts[a].at[span((1 - core) * 2 * own, 2 * own)], kv_near.at[a], place.mate)
        )
        to_across.append(Wire(sems, kv_half.at[a, span((1 - side) * own, own)], kv_far.at[a], place.across))

    def weight_part(a):
        source = (kt, vt)[a]

        def body(t, _):
            slot = lax.rem(t, 2) * 2 + t // 2
            parts[a][span(slot * own, own)] = nn(source[span(t * own, own)], enc[...]).astype(BF)
            return 0

        lax.fori_loop(0, 4, body, 0)
        to_mate[a].start()

    def pass_across(a):
        to_mate[a].wait()
        mine = span(core * 2 * own, 2 * own)
        kv_half[a] = (parts[a][mine].astype(F32) + kv_near[a].astype(F32)).astype(BF)
        to_across[a].start()

    s4.two()
    weight_part(0)
    poll()
    s4.three()
    pass_across(0)
    weight_part(1)
    s4.four()
    poll()
    d_cross = tn(s4.out[...], wq[...])
    pass_across(1)
    dv, gain_grad = norm_back(x2[...], gain_cross, d_cross)
    small[1:2, :width] = gain_grad
    g1, g1_low = scr.g1, scr.g1_low
    g1[...] = g2[...] + dv
    g1_low[...] = g1[...].astype(BF)
    g_small[own : 2 * own] = nn(s4.out[span(me * own, own)], cross_in[...]).astype(BF)
    g_small[2 * own : 3 * own] = nn(att_self[...], g1_low[...]).astype(BF)
    poll()
    d_att_self = nt(ins.wo_self[...], g1_low[...]).astype(BF)
    d_qkv = scr.d_qkv
    for h in range(heads):
        at = slice(h * DH, (h + 1) * DH)
        q = qkv[h * DH : (h + 1) * DH]
        k = qkv[own + h * DH : own + (h + 1) * DH]
        v = qkv[2 * own + h * DH : 2 * own + (h + 1) * DH]
        p = scr.p_self[h]
        grad = tn(v, d_att_self[at])
        ds = (p * (grad - jnp.sum(p * grad, axis=0, keepdims=True))).astype(BF)
        scr.ds_self[h] = ds.astype(F32)
        d_qkv[h * DH : (h + 1) * DH] = nn(k, ds).astype(BF)
        d_qkv[own + h * DH : own + (h + 1) * DH] = nt(q, ds).astype(BF)
        d_qkv[2 * own + h * DH : 2 * own + (h + 1) * DH] = nt(d_att_self[at], p.astype(BF)).astype(BF)
    poll()
    g_small[3 * own : 6 * own] = nn(d_qkv[...], self_in[...]).astype(BF)
    poll()
    s5 = tensor_sum(scr.s5)
    total = None
    for k, weight in enumerate(self_weights):
        part = tn(d_qkv[k * own : (k + 1) * own], weight[...])
        total = part if total is None else total + part
    s5.src[...] = total.astype(BF)
    s5.one()
    poll()
    rows_ref = scr.bucket_rows

    def count(b, _):
        hit = bucket[...] == b
        for h in range(heads):
            value = jnp.where(hit, scr.ds_self[h], 0.0)
            rows_ref[pl.ds(h * buckets + b, 1)] = jnp.sum(value, axis=0, keepdims=True)
        return 0

    s5.two()
    rows_ref[...] = jnp.zeros(rows_ref.shape, F32)
    lax.fori_loop(0, buckets, count, 0)
    position = jnp.sum(rows_ref[...].T, axis=0, keepdims=True)
    for g in range(cfg.groups):
        hot = jnp.where(group == g, 1.0, 0.0).astype(F32)
        small[8 + g : 9 + g, :tokens] = position * hot
    poll()

    saves = [None, None]

    def encoder_tile(r):
        at = slice(r * TILE, (r + 1) * TILE)
        slot = r % 2
        if saves[slot] is not None:
            saves[slot].wait()
        stage = scr.stage.at[slot]
        stage[...] = (nn(kc[at], wk[...]) + nn(vc[at], wv[...])).astype(BF)
        saves[slot] = fetch(stage, outs.encoder_grad.at[pl.ds(r * TILE, TILE)])

    for r in range(tiles // 2):
        encoder_tile(r)
        poll()
    for a in range(2):
        to_across[a].wait()
        g_small[(6 + a) * own : (7 + a) * own] = (
            kv_half[a, span(side * own, own)].astype(F32) + kv_far[a].astype(F32)
        ).astype(BF)
    poll()
    s5.three()
    for r in range(tiles // 2, tiles):
        encoder_tile(r)
        poll()
    s5.four()
    dv, gain_grad = norm_back(xv, gain_self, s5.out[...].astype(F32))
    outs.decoder_grad[...] = (g1[...] + dv).astype(BF)
    small[0:1, :width] = gain_grad
    for copy in saves:
        copy.wait()
    if summing:
        little = SmallSum(sems, place, scr.small)
        little.s0()
        poll()
        little.s1()
        poll()
        little.s2()
        poll()
        little.s3()
        poll()
        little.s4()
        outs.small_sum[...] = little.bufs[6][...]
        poll()
        for chunk in chunks:
            chunk.finish()
    else:
        for copy in [fetch(src, dst) for src, dst in zip(scr.grads, outs.grads)]:
            copy.wait()
        outs.small_sum[...] = small[...]
    for gather in gathers:
        gather.end()


def finish_kernel(own, buckets, heads, groups, ins, outs, scr):
    used = [0]

    def copy(src, dst):
        made = pltpu.make_async_copy(src, dst, scr.sems.at[used[0]])
        used[0] += 1
        made.start()
        return made

    loads = [copy(src, dst) for src, dst in zip(ins.grads, scr.low)]
    keeps = [copy(src, dst) for src, dst in zip(ins.kept, outs.kept)]
    for k in range(3):
        outs.gains[k][...] = ins.little[k : k + 1].reshape(outs.gains[k].shape)
    for h in range(heads):
        outs.position[h] = ins.little[8 : 8 + groups, h * buckets : (h + 1) * buckets]
    for k in range(3):
        loads[k].wait()
        scr.wide[k][...] = scr.low[k][...].astype(F32)
        keeps.append(copy(scr.wide[k], outs.wide[k]))
    loads[3].wait()
    for k, out in enumerate(outs.pieces):
        at = slice(k * own, (k + 1) * own)
        scr.wide[3][at] = scr.low[3][at].astype(F32)
        keeps.append(copy(scr.wide[3].at[at], out))
    for made in keeps:
        made.wait()


def shards(
    mesh_shape,
    decoder_in,
    encoder_out,
    out_grad,
    group_ids,
    target_mask,
    bucket_ids,
    gain_self,
    gain_cross,
    gain_ffn,
    query_self,
    key_self,
    value_self,
    output_self,
    query_cross,
    key_cross,
    value_cross,
    output_cross,
    gate_weight,
    up_weight,
    down_weight,
    position_bias,
):
    dp_size, tensor_size = mesh_shape
    query_count, tokens, width = decoder_in.shape
    assert query_count == 1 and tensor_size == 4 and dp_size % 2 == 0
    heads = query_self.shape[1] // DH
    own, all_heads = heads * DH, heads * tensor_size
    groups, buckets, _ = position_bias.shape
    rows, units = encoder_out.shape[1], gate_weight.shape[1]
    summing = dp_size == 8

    def vmem(*shape, kind=BF):
        return pltpu.VMEM(shape, kind)

    def shape_of(*shape, kind=BF):
        return jax.ShapeDtypeStruct(shape, kind)

    inputs = dict(
        x=(decoder_in[0], VMEM),
        out_grad=(out_grad[0], VMEM),
        encoder=(encoder_out[0], ANY),
        group=(group_ids, SMEM),
        mask=(target_mask, VMEM),
        bucket=(bucket_ids, VMEM),
        gains=[(gain_self, VMEM), (gain_cross, VMEM), (gain_ffn, VMEM)],
        wq_self=(query_self.T, VMEM),
        wk_self=(key_self.T, VMEM),
        wv_self=(value_self.T, VMEM),
        wo_self=(output_self, VMEM),
        wq_cross=(query_cross.T, VMEM),
        wk_cross=(key_cross.T, VMEM),
        wv_cross=(value_cross.T, VMEM),
        wo_cross=(output_cross, VMEM),
        gate_w=(gate_weight, ANY),
        up_w=(up_weight, ANY),
        down_w=(down_weight, ANY),
        table=(jnp.transpose(position_bias, (2, 0, 1)), SMEM),
    )
    grad_shapes = [(units, width), (width, units), (width, units), (8 * own, width)]
    outputs = dict(
        block_out=(shape_of(tokens, width), VMEM),
        decoder_grad=(shape_of(tokens, width), VMEM),
        encoder_grad=(shape_of(rows, width), ANY),
        grads=[(shape_of(*shape), ANY) for shape in grad_shapes],
        small_sum=(shape_of(16, width, kind=F32), VMEM),
    )
    plan = chunk_plan(own, width, units)
    all_own = all_heads * DH

    def sum_bufs(count, lanes):
        return [vmem(size, lanes) for size in (count, count // 2, count // 2, count // 2, count)]

    def chunk_bufs(in_x, source, size):
        lanes = grad_shapes[source][1]
        full = () if in_x else (0, 4)
        return [vmem(size if k in full else size // 2, lanes) for k in range(5)]

    token_low, token_wide = vmem(tokens, width), vmem(tokens, width, kind=F32)
    stats = vmem(16, tokens, kind=F32)
    halves = vmem(all_own // 2, tokens)
    scratch = dict(
        enc=vmem(rows, width), down=vmem(units, width), gate_w=vmem(width, units), up_w=vmem(width, units),
        self_in=token_low, cross_in=token_low, ffn_in=token_low, g1_low=token_low, g2_low=token_low,
        x2=token_wide, x3=token_wide, g1=token_wide, g2=token_wide,
        qkv=vmem(3 * own, tokens), d_qkv=vmem(3 * own, tokens), att_self=vmem(own, tokens),
        bucket=vmem(tokens, tokens, kind=jnp.int32), bucket_rows=vmem(128, tokens, kind=F32),
        p_self=vmem(heads, tokens, tokens, kind=F32), ds_self=vmem(heads, tokens, tokens, kind=F32),
        wk=vmem(all_own, width), wq=vmem(all_own, width), wv=vmem(all_own, width), wo=vmem(all_own, width),
        bq=vmem(all_own, 2 * tokens), bw=vmem(all_own, 2 * tokens),
        kc=vmem(rows, all_own), vc=vmem(rows, all_own), kt=vmem(all_own, rows), vt=vmem(all_own, rows),
        e=vmem(rows, all_heads * tokens), s=vmem(rows, 2 * tokens, kind=F32),
        mix=vmem(all_own, tokens), att=vmem(all_own, tokens), stat=stats, top=stats, lse=stats,
        mix_bufs=[halves] * 3 + [vmem(8, tokens, kind=F32)] * 3,
        delta=vmem(8, 2 * tokens, kind=F32),
        d_hidden=vmem(tokens, units, kind=F32), hidden=vmem(tokens, units),
        d_gate=vmem(tokens, units), d_up=vmem(tokens, units),
        s1=sum_bufs(tokens, width), s3=sum_bufs(tokens, width), so=sum_bufs(tokens, width),
        s4=sum_bufs(all_own, tokens), s5=sum_bufs(tokens, width),
        parts=[vmem(all_own, width)] * 2, kv_near=vmem(2, 2 * own, width),
        kv_half=vmem(2, 2 * own, width), kv_far=vmem(2, own, width),
        stage=vmem(2, TILE, width),
        grads=[vmem(*shape) for shape in grad_shapes],
        small=[vmem(16, width, kind=F32)] * (7 if summing else 1),
        chunks=[chunk_bufs(in_x, source, size) for in_x, source, _, size in plan] if summing else [],
        sems=pltpu.SemaphoreType.DMA((320,)),
    )
    pair = lambda entry: isinstance(entry, tuple)
    first = lambda tree: jax.tree.map(lambda entry: entry[0], tree, is_leaf=pair)
    second = lambda tree: jax.tree.map(lambda entry: entry[1], tree, is_leaf=pair)
    flat = jax.tree.leaves
    trees = [jax.tree.structure(first(inputs)), jax.tree.structure(first(outputs)), jax.tree.structure(scratch)]
    cfg = SimpleNamespace(
        trees=trees, heads=heads, all_heads=all_heads, width=width, tokens=tokens, rows=rows,
        buckets=buckets, groups=groups, summing=summing, chunks=plan, schedule=SCHEDULE,
    )
    result = pl.pallas_call(
        functools.partial(block_kernel, cfg),
        out_shape=flat(first(outputs)),
        in_specs=flat(second(inputs)),
        out_specs=flat(second(outputs)),
        scratch_shapes=flat(scratch),
        compiler_params=pltpu.CompilerParams(collective_id=0, has_side_effects=True, vmem_limit_bytes=63 << 20),
        name="block",
    )(*flat(first(inputs)))
    got = SimpleNamespace(**jax.tree.unflatten(trees[1], result))
    kept = [got.block_out, got.decoder_grad, got.encoder_grad]
    if summing:
        inputs = dict(grads=got.grads, kept=kept, little=got.small_sum)
        outputs = dict(
            kept=[shape_of(*value.shape) for value in kept],
            gains=[shape_of(width, kind=F32)] * 3,
            position=shape_of(heads, groups, buckets, kind=F32),
            wide=[shape_of(*shape, kind=F32) for shape in grad_shapes[:3]],
            pieces=[shape_of(own, width, kind=F32)] * 8,
        )
        scratch = dict(
            low=[vmem(*shape) for shape in grad_shapes],
            wide=[vmem(*shape, kind=F32) for shape in grad_shapes],
            sems=pltpu.SemaphoreType.DMA((32,)),
        )
        trees = [jax.tree.structure(inputs), jax.tree.structure(outputs), jax.tree.structure(scratch)]

        def finish(*refs):
            groups_of, at = [], 0
            for tree in trees:
                groups_of.append(SimpleNamespace(**jax.tree.unflatten(tree, refs[at : at + tree.num_leaves])))
                at += tree.num_leaves
            finish_kernel(own, buckets, heads, groups, *groups_of)

        specs_in = dict(grads=[ANY] * 4, kept=[ANY] * 3, little=VMEM)
        specs_out = dict(kept=[ANY] * 3, gains=[VMEM] * 3, position=VMEM, wide=[ANY] * 3, pieces=[ANY] * 8)
        result = pl.pallas_call(
            finish,
            out_shape=flat(outputs),
            in_specs=flat(specs_in),
            out_specs=flat(specs_out),
            scratch_shapes=flat(scratch),
            compiler_params=pltpu.CompilerParams(vmem_limit_bytes=63 << 20),
            name="finish",
        )(*flat(inputs))
        done = SimpleNamespace(**jax.tree.unflatten(trees[1], result))
        kept, gain_grads, position = done.kept, done.gains, jnp.transpose(done.position, (1, 2, 0))
        wide, pieces = done.wide, done.pieces
    else:
        sums, little = lax.psum(([value.astype(F32) for value in got.grads], got.small_sum), "dp")
        wide = sums[:3]
        pieces = [sums[3][k * own : (k + 1) * own] for k in range(8)]
        gain_grads = [little[k] for k in range(3)]
        position = little[8 : 8 + groups, : heads * buckets].reshape(groups, heads, buckets)
        position = jnp.transpose(position, (0, 2, 1))
    down, gate, up = wide
    oc, qc, os, qs, ks, vs, kc, vc = pieces
    return (
        *[value[None] for value in kept], *gain_grads,
        qs.T, ks.T, vs.T, os, qc.T, kc.T, vc.T, oc, gate, up, down, position,
    )


def solution(mesh):
    rows = P("dp", None, None)
    encoder = P("dp", "tensor", None)
    columns, lines, whole = P(None, "tensor"), P("tensor", None), P()
    head_table = P(None, None, "tensor")
    weights = (columns, columns, columns, lines, columns, columns, columns, lines, columns, columns, lines, head_table)
    return jax.shard_map(
        functools.partial(shards, (mesh.shape["dp"], mesh.shape["tensor"])),
        mesh=mesh,
        in_specs=(rows, encoder, rows, P("dp"), P("dp", None), whole, whole, whole, whole) + weights,
        out_specs=(rows, rows, encoder, whole, whole, whole) + weights,
        check_vma=False,
    )
```

time: 732 us -> 241 us (0.33)
  waiting for transfers between devices: 511 us -> 0 us
  Pallas kernels: 0 us -> 239 us
  matrix products: 88.8 us -> 0 us
  blocking collectives: 61.5 us -> 0 us
  other arithmetic: 30.2 us -> 0 us
  local copies, waits for them, and re-layouts: 22.4 us -> 0 us
  between operations: 15.4 us -> 1.48 us
    psum x6 -> x0, waiting for transfers between devices: 401 us -> none  [the longest x1 273 us: shards(): lax.psum((grad_gain_self, grad_gain_cross, grad_gain_ffn, grad_query_self...]
    pallas_call x0 -> x2, Pallas kernels: none -> 239 us  [the longest x1 153 us: shards(): pl.pallas_call(functools.partial(block_kernel, cfg), out_shape=flat(first...]
    dot_general x48 -> x0, matrix products: 88.8 us -> none  [the longest x9 12.9 us: matmul_left_t(): lax.dot_general(left, right, (((0,), (0,)), ((), ())), preferred_element_...]
    reduce_scatter x4 -> x0, waiting for transfers between devices: 79.7 us -> none  [the longest x1 26.7 us: shards(): lax.psum_scatter(value_part.astype(jnp.bfloat16), 'tensor', scatter_dimen...]
    psum x2 -> x0, blocking collectives: 45.4 us -> none  [the longest x1 38.7 us: shards(): lax.psum((grad_gain_self, grad_gain_cross, grad_gain_ffn, grad_query_self...]
    all_gather x3 -> x0, waiting for transfers between devices: 28.9 us -> none  [the longest x1 14.9 us: shards(): lax.all_gather(output_cross, 'tensor', axis=0, tiled=True)]
    unnamed x146 -> x0, local copies, waits for them, and re-layouts: 19.6 us -> none
    all_gather x3 -> x0, blocking collectives: 16.1 us -> none  [the longest x2 10.5 us: merged(): everything = jax.tree.map(lambda part: lax.all_gather(part, axis), shard)]
  transfers between devices with their start and end apart: 13 -> 0, of which waited for: 13 -> 0; matrix products, arithmetic and copies ran while one was open for 9% -> 0% of each run, Pallas kernels for 0% -> 0%
where the time goes in v2:
time: 241 us
  Pallas kernels  239 us (99%)
    pallas_call x1, Pallas kernels, shards(): pl.pallas_call(functools.partial(block_kernel, cfg), out_shape=flat(first...  153 us
    pallas_call x1, Pallas kernels, shards(): pl.pallas_call(finish, out_shape=flat(outputs), in_specs=flat(specs_in),...  86.2 us

profile of v2, /device:TPU:0, one launch (start us, length us, event | category | flops | bytes accessed | tf_op | source)
XLA Modules:
  0.0 240.6 jit_solution(7617562978812508891)
XLA Ops:
  1.3 152.9 %block.1 = (bf16[128,768]{1,0:T(8,128)(2,1)}, bf16[128,768]{1,0:T(8,128)(2,1)}, bf16[1536,768]{1,0:T(8,128)(2,1)}, bf16[512,768]{1,0:T(8,128)(2,1)}, bf16[768,51...) custom-call(s32[128,128]{1,0:T(8,128)} %refs_0_.1, ...), custom_call_target="tpu_custom_call" | custom-call | tf_op jit(solution)/shard_map/block/pallas_call | solution.py:1068
  154.3 86.2 %finish.1 = (f32[768]{0:T(1024)}, f32[768]{0:T(1024)}, f32[768]{0:T(1024)}, bf16[128,768]{1,0:T(8,128)(2,1)}, bf16[128,768]{1,0:T(8,128)(2,1)}, /*index=5*/bf16[...) custom-call(bf16[512,768]{1,0:T(8,128)(2,1)} %get-tuple-element.44.r, ...), custom_call_target="tpu_custom_call" | custom-call | tf_op jit(solution)/shard_map/finish/pallas_call | solution.py:1104

commit v3 on v2

--- a/solution.py
+++ b/solution.py
@@ -22,41 +22,43 @@
 GELU_CUBIC = 0.044715
 
 
-IN_X = (True, True, True, False, False, True, False, True, False, True, True, True, True, False)
+IN_X = (True, True, True, True, True, False, True, False, True, True, True, True, True, False)
 SCHEDULE = (
-    ((0, 0),),
+    (),
     ((3, 0),),
-    (),
+    ((2, 0), (5, 0),),
+    ((4, 0),),
+    (),
+    ((3, 1),),
+    (),
+    ((2, 1), (6, 0), (5, 1),),
     ((1, 0),),
-    ((0, 1),),
-    ((2, 0),),
-    ((1, 1), (3, 1),),
-    ((5, 0),),
-    (),
-    ((0, 2), (2, 1),),
-    ((3, 2),),
-    ((1, 2), (5, 1),),
-    ((4, 0), (0, 3),),
-    ((2, 2), (3, 3),),
-    ((1, 3),),
-    ((0, 4), (2, 3),),
-    ((4, 1), (1, 4), (6, 0),),
-    ((3, 4), (7, 0), (0, 5),),
-    ((5, 2),),
-    (),
-    ((4, 2), (1, 5), (9, 0), (8, 0),),
-    ((2, 4),),
-    ((7, 1), (6, 1), (5, 3),),
-    ((3, 5),),
-    ((4, 3), (10, 0),),
-    ((6, 2), (8, 1), (5, 4),),
-    ((2, 5),),
-    ((7, 2), (4, 4), (13, 0),),
-    ((9, 1),),
-    ((9, 2), (11, 0), (8, 2), (6, 3),),
-    ((5, 5), (7, 3), (12, 0), (4, 5),),
-    ((10, 1), (13, 1), (9, 3),),
-    ((8, 3), (10, 2), (6, 4), (7, 4), (13, 2), (9, 4), (7, 5), (8, 4), (6, 5), (11, 1), (11, 2), (9, 5), (10, 3), (12, 1), (12, 2), (8, 5), (11, 3), (10, 4), (12, 3), (13, 3), (11, 4), (10, 5), (12, 4), (13, 4), (11, 5), (12, 5), (13, 5),),
+    ((0, 0), (3, 2), (4, 1),),
+    (),
+    (),
+    ((5, 2), (3, 3), (4, 2), (2, 2), (1, 1), (6, 1),),
+    (),
+    (),
+    ((4, 3), (1, 2),),
+    ((2, 3), (5, 3), (3, 4),),
+    ((6, 2), (0, 1), (12, 0),),
+    (),
+    ((8, 0), (5, 4),),
+    (),
+    ((0, 2), (9, 0), (7, 0),),
+    (),
+    ((1, 3), (7, 1), (2, 4), (0, 3), (12, 1),),
+    ((4, 4), (12, 2),),
+    (),
+    ((8, 1), (8, 2), (13, 0), (7, 2), (10, 0), (11, 0), (6, 3), (9, 1), (12, 3), (2, 5), (13, 1), (0, 4), (6, 4), (1, 4), (7, 3), (13, 2), (8, 3), (5, 5), (9, 2),),
+    ((7, 4), (3, 5), (10, 1), (10, 2), (11, 1), (9, 3), (8, 4), (12, 4), (11, 2), (10, 3),),
+    (),
+    ((9, 4),),
+    (),
+    ((11, 3), (6, 5), (10, 4), (12, 5), (11, 4),),
+    ((4, 5),),
+    (),
+    ((13, 3), (13, 4), (0, 5), (9, 5), (13, 5), (7, 5), (1, 5), (8, 5), (11, 5), (10, 5),),
 )
 
 
@@ -250,6 +252,34 @@
 
     def end(self):
         for wire in (self.across, self.mate, self.side, self.direct, self.relayed):
+            wire.sent()
+
+
+class QueryGather:
+    def __init__(self, sems, place, own, whole):
+        rows = own.shape[0]
+        there = (1 - place.side) * 2 + place.core
+        self.own, self.whole, self.mine = own, whole, span(place.me * rows, rows)
+        self.across = Wire(sems, own, whole.at[self.mine], place.across)
+        self.mate = Wire(sems, own, whole.at[self.mine], place.mate)
+        theirs = whole.at[span(there * rows, rows)]
+        self.onward = Wire(sems, theirs, theirs, place.mate)
+
+    def one(self):
+        self.across.start()
+        self.mate.start()
+        self.whole[self.mine] = self.own[...]
+
+    def two(self):
+        self.across.came()
+        self.onward.start()
+
+    def three(self):
+        self.mate.came()
+        self.onward.came()
+
+    def end(self):
+        for wire in (self.across, self.mate, self.onward):
             wire.sent()
 
 
@@ -512,14 +542,21 @@
         return copy
 
     enc, down, gate_w, up_w = scr.enc, scr.down, scr.gate_w, scr.up_w
+    first_loads = [fetch(ins.x, scr.x)]
+    self_weights = scr.wqkv
+    for src, dst in zip((ins.wq_self, ins.wk_self, ins.wv_self), self_weights):
+        first_loads.append(fetch(src, dst))
+    load_bucket, load_out = fetch(ins.bucket, scr.bucket), fetch(ins.wo_self, scr.wo_self)
+    load_query = fetch(ins.wq_cross, scr.wq_own)
     load_enc = fetch(ins.encoder, enc)
-    load_ffn = [fetch(ins.down_w, down), fetch(ins.gate_w, gate_w), fetch(ins.up_w, up_w)]
-
-    xv = ins.x[...].astype(F32)
+    load_ffn = [fetch(ins.out_grad, scr.og), fetch(ins.down_w, down), fetch(ins.gate_w, gate_w), fetch(ins.up_w, up_w)]
+
+    for load in first_loads:
+        load.wait()
+    xv = scr.x[...].astype(F32)
     self_in = scr.self_in
     self_in[...] = (xv * rms_scale(xv) * gain_self).astype(BF)
     qkv = scr.qkv
-    self_weights = (ins.wq_self, ins.wk_self, ins.wv_self)
     for k, weight in enumerate(self_weights):
         qkv[k * own : (k + 1) * own] = nt(weight[...], self_in[...]).astype(BF)
     if summing:
@@ -532,8 +569,8 @@
         for part, whole in ((ins.wk_cross, wk), (ins.wq_cross, wq), (ins.wv_cross, wv), (ins.wo_cross, wo))
     ]
     get_k.start()
-    get_q.start()
-    scr.bucket[...] = ins.bucket[...].T
+    load_bucket.wait()
+    scr.bucket[...] = scr.bucket[...].T
     bucket = scr.bucket
     keep = jnp.broadcast_to(ins.mask[...].astype(F32), (tokens, tokens)).T
     j_at = lax.broadcasted_iota(jnp.int32, (tokens, tokens), 0)
@@ -551,7 +588,6 @@
         return 0
 
     lax.fori_loop(0, buckets, spread, 0)
-    get_v.start()
     att_self = scr.att_self
 
     def attend(h):
@@ -564,63 +600,56 @@
         scr.p_self[h] = p
         att_self[h * DH : (h + 1) * DH] = nn(v, p.astype(BF)).astype(BF)
 
-    attend(0)
-    get_o.start()
-    for h in range(1, heads):
+    for h in range(heads):
         attend(h)
-    get_k.one()
 
     def tensor_sum(bufs):
         return TensorSum(sems, place, *bufs)
 
     s1 = tensor_sum(scr.s1)
-    s1.src[...] = tn(att_self[...], ins.wo_self[...]).astype(BF)
+    load_out.wait()
+    s1.src[...] = tn(att_self[...], scr.wo_self[...]).astype(BF)
     s1.one()
-    get_q.one()
-    get_k.two()
     s1.two()
-    get_v.one()
-    get_q.two()
-    get_o.one()
-    get_v.two()
+    get_v.start()
+    get_k.one()
     load_enc.wait()
-    get_k.three()
-    kc, vc, kt, vt, e_ref = scr.kc, scr.vc, scr.kt, scr.vt, scr.e
-
-    def project(dst, weight):
+    kc, vc, e_ref = scr.kc, scr.vc, scr.e
+
+    def project(dst, weight, first, count):
+        lanes = span(first, count, 2 * DH)
+
         def body(r, _):
             at = span(r * TILE, TILE)
-            dst[at] = nt(enc[at], weight[...]).astype(BF)
+            dst[at, lanes] = nt(enc[at], weight[lanes]).astype(BF)
             return 0
 
         lax.fori_loop(0, tiles, body, 0)
 
-    def project_t(dst, weight):
-        def body(r, _):
-            at = span(r * TILE, TILE)
-            dst[:, at] = nt(weight[...], enc[at]).astype(BF)
-            return 0
-
-        lax.fori_loop(0, tiles, body, 0)
-
-    project(kc, wk)
     s1.three()
-    get_o.two()
-    get_v.three()
-    project_t(vt, wv)
     s1.four()
     x2 = scr.x2
-    x2[...] = xv + s1.out[...].astype(F32)
+    x2[...] = scr.x[...].astype(F32) + s1.out[...].astype(F32)
     cross_in = scr.cross_in
     cross_in[...] = (x2[...] * rms_scale(x2[...]) * gain_cross).astype(BF)
-    get_q.three()
+    load_query.wait()
+    scr.q_own[...] = nt(scr.wq_own[...], cross_in[...]).astype(BF)
+    get_query = QueryGather(sems, place, scr.q_own, scr.q_t)
+    get_query.one()
+    get_o.start()
+    get_q.start()
+    get_k.two()
+    get_v.one()
+    get_k.three()
+    project(kc, wk, 0, all_heads * DH)
+    get_query.two()
     bq, bw = scr.bq, scr.bw
     bq[...] = jnp.zeros(bq.shape, BF)
     bw[...] = jnp.zeros(bw.shape, BF)
-    q_t = nt(wq[...], cross_in[...]).astype(BF)
+    get_query.three()
     for h in range(all_heads):
         at = slice(h * DH, (h + 1) * DH)
-        bq[at, (h % 2) * tokens : (h % 2 + 1) * tokens] = q_t[at]
+        bq[at, (h % 2) * tokens : (h % 2 + 1) * tokens] = scr.q_t[at]
     s_ref, mix, stat, top_ref = scr.s, scr.mix, scr.stat, scr.top
     stat[...] = jnp.zeros(stat.shape, F32)
     top_ref[...] = jnp.zeros(top_ref.shape, F32)
@@ -629,7 +658,7 @@
     def stat_row(p):
         return (p // per_half) * 8 + 2 * (p - (p // per_half) * per_half)
 
-    def forward_pair(p, _):
+    def score_pair(p, _):
         head_at = span(p * 2 * DH, 2 * DH)
         score_at = span(p * 2 * tokens, 2 * tokens)
         weights = bq[head_at]
@@ -641,38 +670,51 @@
             part = fold(s, jnp.max)
             top = part if top is None else jnp.maximum(top, part)
         top = jnp.max(top, axis=0, keepdims=True)
-        total, acc = None, None
+        total = None
         for r in range(tiles):
             at = slice(r * TILE, (r + 1) * TILE)
             e = jnp.exp(s_ref[at] - top)
             part = fold(e, jnp.sum)
             total = part if total is None else total + part
-            low = e.astype(BF)
-            e_ref[at, score_at] = low
-            part = nn(vt[head_at, at], low)
-            acc = part if acc is None else acc + part
+            e_ref[at, score_at] = e.astype(BF)
         total = jnp.sum(total, axis=0, keepdims=True)
-        inverse = 1.0 / total
+        scr.inverse[pl.ds(p, 1)] = 1.0 / total
         lse = top + jnp.log(total)
         row = stat_row(p)
         for k in range(2):
             lanes = slice(k * tokens, (k + 1) * tokens)
-            value = acc[k * DH : (k + 1) * DH, lanes] * inverse[:, lanes]
-            mix[span(p * 2 * DH + k * DH, DH)] = value.astype(BF)
             stat[pl.ds(row + k, 1)] = lse[:, lanes]
             top_ref[pl.ds(row + k, 1)] = top[:, lanes]
         return 0
 
-    lax.fori_loop(0, pairs, forward_pair, 0)
+    def mix_pair(p, _):
+        acc = tn(vc[:, span(p * 2 * DH, 2 * DH)], e_ref[:, span(p * 2 * tokens, 2 * tokens)])
+        inverse = scr.inverse[pl.ds(p, 1)]
+        for k in range(2):
+            lanes = slice(k * tokens, (k + 1) * tokens)
+            value = acc[k * DH : (k + 1) * DH, lanes] * inverse[:, lanes]
+            mix[span(p * 2 * DH + k * DH, DH)] = value.astype(BF)
+        return 0
+
+    lax.fori_loop(0, pairs - 2, score_pair, 0)
+    get_v.two()
+    lax.fori_loop(pairs - 2, pairs, score_pair, 0)
+    get_o.one()
+    get_v.three()
     att, lse = scr.att, scr.lse
     s2 = TensorMix(sems, place, mix, stat, scr.mix_bufs, att, lse)
-    s2.one()
+    for half in (1 - core, core):
+        project(vc, wv, half * per_half * 2 * DH, per_half * 2 * DH)
+        lax.fori_loop(half * per_half, (half + 1) * per_half, mix_pair, 0)
+        if half is not core:
+            s2.one()
+            get_q.one()
+    s2.two()
     for load in load_ffn:
         load.wait()
-    og = ins.out_grad
+    og = scr.og
     scr.d_hidden[...] = nt(og[...], down[...]).astype(BF).astype(F32)
-    s2.two()
-    project(vc, wv)
+    get_o.two()
     s2.three()
     get_o.three()
     s2.four()
@@ -720,7 +762,7 @@
     so.src[...] = nn(scr.hidden[...], down[...]).astype(BF)
     s3.two()
     poll()
-    project_t(kt, wk)
+    get_q.two()
     poll()
     s3.three()
     so.one()
@@ -762,60 +804,78 @@
             e = e_ref[at, score_at]
             grad = nn(vc[at, head_at], wa_block)
             ds = (e.astype(F32) * (grad - delta)).astype(BF)
-            part = nn(kt[head_at, at], ds)
+            part = tn(kc[at, head_at], ds)
             acc = part if acc is None else acc + part
             kc[at, head_at] = nt(ds, wq_block).astype(BF)
             vc[at, head_at] = nt(e, wa_block).astype(BF)
-            kt[head_at, at] = nt(wq_block, ds).astype(BF)
-            vt[head_at, at] = nt(wa_block, e).astype(BF)
         for k in range(2):
             value = acc[k * DH : (k + 1) * DH, k * tokens : (k + 1) * tokens]
             s4.src[span(p * 2 * DH + k * DH, DH)] = value.astype(BF)
         return 0
 
-    for p in range(pairs):
-        poll()
-        lax.fori_loop(p, p + 1, backward_pair, 0)
-    s4.one()
-    so.four()
-    outs.block_out[...] = (x3[...] + so.out[...].astype(F32)).astype(BF)
-    poll()
-
-    parts, kv_near, kv_half, kv_far = scr.parts, scr.kv_near, scr.kv_half, scr.kv_far
-    to_mate, to_across = [], []
+    far_at, near_at = (1 - side) * per_half, side * per_half
+    far_parts, near_parts = scr.far_parts, scr.near_parts
+    kv_near, kv_home, kv_half, kv_far = scr.kv_near, scr.kv_home, scr.kv_half, scr.kv_far
+    to_mate, to_across, to_home = [], [], []
+    mine, other = span(core * own, own), span((1 - core) * own, own)
     for a in range(2):
-        to_mate.append(
-            Wire(sems, parts[a].at[span((1 - core) * 2 * own, 2 * own)], kv_near.at[a], place.mate)
-        )
-        to_across.append(Wire(sems, kv_half.at[a, span((1 - side) * own, own)], kv_far.at[a], place.across))
-
-    def weight_part(a):
-        source = (kt, vt)[a]
+        to_mate.append(Wire(sems, far_parts[a].at[other], kv_near.at[a], place.mate))
+        to_across.append(Wire(sems, kv_half.at[a], kv_far.at[a], place.across))
+        to_home.append(Wire(sems, near_parts[a].at[other], kv_home.at[a], place.mate))
+
+    def weight_part(dst, source, first):
+        rows_of = source[:, span(first * 2 * DH, 2 * own, 2 * DH)]
 
         def body(t, _):
-            slot = lax.rem(t, 2) * 2 + t // 2
-            parts[a][span(slot * own, own)] = nn(source[span(t * own, own)], enc[...]).astype(BF)
+            lanes = span(t * TILE, TILE)
+            dst[:, lanes] = tn(rows_of, enc[:, lanes]).astype(BF)
             return 0
 
-        lax.fori_loop(0, 4, body, 0)
-        to_mate[a].start()
+        lax.fori_loop(0, width // TILE, body, 0)
 
     def pass_across(a):
         to_mate[a].wait()
-        mine = span(core * 2 * own, 2 * own)
-        kv_half[a] = (parts[a][mine].astype(F32) + kv_near[a].astype(F32)).astype(BF)
+        kv_half[a] = (far_parts[a][mine].astype(F32) + kv_near[a].astype(F32)).astype(BF)
         to_across[a].start()
 
+    for p in range(per_half):
+        poll()
+        lax.fori_loop(far_at + p, far_at + p + 1, backward_pair, 0)
+    poll()
+    so.four()
+    scr.out_stage[...] = (x3[...] + so.out[...].astype(F32)).astype(BF)
+    token_saves = [fetch(scr.out_stage, outs.block_out)]
+    weight_part(far_parts[0], kc, far_at)
+    to_mate[0].start()
+    weight_part(far_parts[1], vc, far_at)
+    to_mate[1].start()
+    pass_across(0)
+    for p in range(per_half):
+        poll()
+        lax.fori_loop(near_at + p, near_at + p + 1, backward_pair, 0)
+    s4.one()
+    poll()
+    weight_part(near_parts[0], kc, near_at)
+    to_home[0].start()
     s4.two()
-    weight_part(0)
-    poll()
+    pass_across(1)
+    poll()
+    weight_part(near_parts[1], vc, near_at)
+    to_home[1].start()
     s4.three()
-    pass_across(0)
-    weight_part(1)
+    poll()
+
+    def kv_done(a):
+        to_home[a].wait()
+        to_across[a].wait()
+        total = near_parts[a][mine].astype(F32) + kv_home[a].astype(F32) + kv_far[a].astype(F32)
+        g_small[(6 + a) * own : (7 + a) * own] = total.astype(BF)
+
+    kv_done(0)
     s4.four()
     poll()
+    get_q.three()
     d_cross = tn(s4.out[...], wq[...])
-    pass_across(1)
     dv, gain_grad = norm_back(x2[...], gain_cross, d_cross)
     small[1:2, :width] = gain_grad
     g1, g1_low = scr.g1, scr.g1_low
@@ -824,7 +884,7 @@
     g_small[own : 2 * own] = nn(s4.out[span(me * own, own)], cross_in[...]).astype(BF)
     g_small[2 * own : 3 * own] = nn(att_self[...], g1_low[...]).astype(BF)
     poll()
-    d_att_self = nt(ins.wo_self[...], g1_low[...]).astype(BF)
+    d_att_self = nt(scr.wo_self[...], g1_low[...]).astype(BF)
     d_qkv = scr.d_qkv
     for h in range(heads):
         at = slice(h * DH, (h + 1) * DH)
@@ -881,21 +941,18 @@
     for r in range(tiles // 2):
         encoder_tile(r)
         poll()
-    for a in range(2):
-        to_across[a].wait()
-        g_small[(6 + a) * own : (7 + a) * own] = (
-            kv_half[a, span(side * own, own)].astype(F32) + kv_far[a].astype(F32)
-        ).astype(BF)
+    kv_done(1)
     poll()
     s5.three()
     for r in range(tiles // 2, tiles):
         encoder_tile(r)
         poll()
     s5.four()
-    dv, gain_grad = norm_back(xv, gain_self, s5.out[...].astype(F32))
-    outs.decoder_grad[...] = (g1[...] + dv).astype(BF)
+    dv, gain_grad = norm_back(scr.x[...].astype(F32), gain_self, s5.out[...].astype(F32))
+    scr.og[...] = (g1[...] + dv).astype(BF)
+    token_saves.append(fetch(scr.og, outs.decoder_grad))
     small[0:1, :width] = gain_grad
-    for copy in saves:
+    for copy in saves + token_saves:
         copy.wait()
     if summing:
         little = SmallSum(sems, place, scr.small)
@@ -916,7 +973,7 @@
         for copy in [fetch(src, dst) for src, dst in zip(scr.grads, outs.grads)]:
             copy.wait()
         outs.small_sum[...] = small[...]
-    for gather in gathers:
+    for gather in gathers + [get_query]:
         gather.end()
 
 
@@ -930,7 +987,8 @@
         return made
 
     loads = [copy(src, dst) for src, dst in zip(ins.grads, scr.low)]
-    keeps = [copy(src, dst) for src, dst in zip(ins.kept, outs.kept)]
+    moves = [copy(src, dst) for src, dst in zip(ins.kept, scr.kept)]
+    keeps = []
     for k in range(3):
         outs.gains[k][...] = ins.little[k : k + 1].reshape(outs.gains[k].shape)
     for h in range(heads):
@@ -944,6 +1002,9 @@
         at = slice(k * own, (k + 1) * own)
         scr.wide[3][at] = scr.low[3][at].astype(F32)
         keeps.append(copy(scr.wide[3].at[at], out))
+    for k, move in enumerate(moves):
+        move.wait()
+        keeps.append(copy(scr.kept[k], outs.kept[k]))
     for made in keeps:
         made.wait()
 
@@ -988,21 +1049,21 @@
         return jax.ShapeDtypeStruct(shape, kind)
 
     inputs = dict(
-        x=(decoder_in[0], VMEM),
-        out_grad=(out_grad[0], VMEM),
+        x=(decoder_in[0], ANY),
+        out_grad=(out_grad[0], ANY),
         encoder=(encoder_out[0], ANY),
         group=(group_ids, SMEM),
         mask=(target_mask, VMEM),
-        bucket=(bucket_ids, VMEM),
+        bucket=(bucket_ids, ANY),
         gains=[(gain_self, VMEM), (gain_cross, VMEM), (gain_ffn, VMEM)],
-        wq_self=(query_self.T, VMEM),
-        wk_self=(key_self.T, VMEM),
-        wv_self=(value_self.T, VMEM),
-        wo_self=(output_self, VMEM),
-        wq_cross=(query_cross.T, VMEM),
-        wk_cross=(key_cross.T, VMEM),
-        wv_cross=(value_cross.T, VMEM),
-        wo_cross=(output_cross, VMEM),
+        wq_self=(query_self.T, ANY),
+        wk_self=(key_self.T, ANY),
+        wv_self=(value_self.T, ANY),
+        wo_self=(output_self, ANY),
+        wq_cross=(query_cross.T, ANY),
+        wk_cross=(key_cross.T, ANY),
+        wv_cross=(value_cross.T, ANY),
+        wo_cross=(output_cross, ANY),
         gate_w=(gate_weight, ANY),
         up_w=(up_weight, ANY),
         down_w=(down_weight, ANY),
@@ -1010,8 +1071,8 @@
     )
     grad_shapes = [(units, width), (width, units), (width, units), (8 * own, width)]
     outputs = dict(
-        block_out=(shape_of(tokens, width), VMEM),
-        decoder_grad=(shape_of(tokens, width), VMEM),
+        block_out=(shape_of(tokens, width), ANY),
+        decoder_grad=(shape_of(tokens, width), ANY),
         encoder_grad=(shape_of(rows, width), ANY),
         grads=[(shape_of(*shape), ANY) for shape in grad_shapes],
         small_sum=(shape_of(16, width, kind=F32), VMEM),
@@ -1028,9 +1089,11 @@
         return [vmem(size if k in full else size // 2, lanes) for k in range(5)]
 
     token_low, token_wide = vmem(tokens, width), vmem(tokens, width, kind=F32)
-    stats = vmem(16, tokens, kind=F32)
+    stats, kv_block = vmem(16, tokens, kind=F32), vmem(2, own, width)
     halves = vmem(all_own // 2, tokens)
     scratch = dict(
+        x=token_low, og=token_low, out_stage=token_low, wqkv=[vmem(own, width)] * 3, wo_self=vmem(own, width), wq_own=vmem(own, width),
+        q_own=vmem(own, tokens), q_t=vmem(all_own, tokens),
         enc=vmem(rows, width), down=vmem(units, width), gate_w=vmem(width, units), up_w=vmem(width, units),
         self_in=token_low, cross_in=token_low, ffn_in=token_low, g1_low=token_low, g2_low=token_low,
         x2=token_wide, x3=token_wide, g1=token_wide, g2=token_wide,
@@ -1039,17 +1102,17 @@
         p_self=vmem(heads, tokens, tokens, kind=F32), ds_self=vmem(heads, tokens, tokens, kind=F32),
         wk=vmem(all_own, width), wq=vmem(all_own, width), wv=vmem(all_own, width), wo=vmem(all_own, width),
         bq=vmem(all_own, 2 * tokens), bw=vmem(all_own, 2 * tokens),
-        kc=vmem(rows, all_own), vc=vmem(rows, all_own), kt=vmem(all_own, rows), vt=vmem(all_own, rows),
+        kc=vmem(rows, all_own), vc=vmem(rows, all_own),
         e=vmem(rows, all_heads * tokens), s=vmem(rows, 2 * tokens, kind=F32),
         mix=vmem(all_own, tokens), att=vmem(all_own, tokens), stat=stats, top=stats, lse=stats,
         mix_bufs=[halves] * 3 + [vmem(8, tokens, kind=F32)] * 3,
-        delta=vmem(8, 2 * tokens, kind=F32),
+        delta=vmem(8, 2 * tokens, kind=F32), inverse=vmem(8, 2 * tokens, kind=F32),
         d_hidden=vmem(tokens, units, kind=F32), hidden=vmem(tokens, units),
         d_gate=vmem(tokens, units), d_up=vmem(tokens, units),
         s1=sum_bufs(tokens, width), s3=sum_bufs(tokens, width), so=sum_bufs(tokens, width),
         s4=sum_bufs(all_own, tokens), s5=sum_bufs(tokens, width),
-        parts=[vmem(all_own, width)] * 2, kv_near=vmem(2, 2 * own, width),
-        kv_half=vmem(2, 2 * own, width), kv_far=vmem(2, own, width),
+        far_parts=[vmem(2 * own, width)] * 2, near_parts=[vmem(2 * own, width)] * 2,
+        kv_near=kv_block, kv_home=kv_block, kv_half=kv_block, kv_far=kv_block,
         stage=vmem(2, TILE, width),
         grads=[vmem(*shape) for shape in grad_shapes],
         small=[vmem(16, width, kind=F32)] * (7 if summing else 1),
@@ -1087,6 +1150,7 @@
         )
         scratch = dict(
             low=[vmem(*shape) for shape in grad_shapes],
+            kept=[vmem(*value.shape) for value in kept],
             wide=[vmem(*shape, kind=F32) for shape in grad_shapes],
             sems=pltpu.SemaphoreType.DMA((32,)),
         )

time: 241 us -> 157 us (0.65)
  Pallas kernels: 239 us -> 155 us
    pallas_call x1, Pallas kernels: 86.2 us -> 8.67 us  [shards(): pl.pallas_call(finish, out_shape=flat(outputs), in_specs=flat(specs_in),...]
    pallas_call x1, Pallas kernels: 153 us -> 147 us  [shards(): pl.pallas_call(functools.partial(block_kernel, cfg), out_shape=flat(first...]
where the time goes in v3:
time: 157 us
  Pallas kernels  155 us (99%)
    pallas_call x1, Pallas kernels, shards(): pl.pallas_call(functools.partial(block_kernel, cfg), out_shape=flat(first...  147 us
    pallas_call x1, Pallas kernels, shards(): pl.pallas_call(finish, out_shape=flat(outputs), in_specs=flat(specs_in),...  8.67 us

profile of v3, /device:TPU:0, one launch (start us, length us, event | category | flops | bytes accessed | tf_op | source)
XLA Modules:
  0.0 156.7 jit_solution(16300076481293685325)
XLA Ops:
  1.3 146.6 %block.1 = (bf16[128,768]{1,0:T(8,128)(2,1)}, bf16[128,768]{1,0:T(8,128)(2,1)}, bf16[1536,768]{1,0:T(8,128)(2,1)}, bf16[512,768]{1,0:T(8,128)(2,1)}, bf16[768,51...) custom-call(s32[128,128]{1,0:T(8,128)} %refs_0_.1, ...), custom_call_target="tpu_custom_call" | custom-call | tf_op jit(solution)/shard_map/block/pallas_call | solution.py:1131
  147.9 8.7 %finish.1 = (f32[768]{0:T(1024)}, f32[768]{0:T(1024)}, f32[768]{0:T(1024)}, bf16[128,768]{1,0:T(8,128)(2,1)}, bf16[128,768]{1,0:T(8,128)(2,1)}, /*index=5*/bf16[...) custom-call(bf16[512,768]{1,0:T(8,128)(2,1)} %get-tuple-element.44.r, ...), custom_call_target="tpu_custom_call" | custom-call | tf_op jit(solution)/shard_map/finish/pallas_call | solution.py:1168

commit v4 on v3

--- a/solution.py
+++ b/solution.py
@@ -22,43 +22,43 @@
 GELU_CUBIC = 0.044715
 
 
-IN_X = (True, True, True, True, True, False, True, False, True, True, True, True, True, False)
+IN_X = (True, True, True, False, True, True, False, True, True)
 SCHEDULE = (
-    (),
-    ((3, 0),),
-    ((2, 0), (5, 0),),
-    ((4, 0),),
-    (),
-    ((3, 1),),
-    (),
-    ((2, 1), (6, 0), (5, 1),),
-    ((1, 0),),
-    ((0, 0), (3, 2), (4, 1),),
+    ((9, 0),),
     (),
     (),
-    ((5, 2), (3, 3), (4, 2), (2, 2), (1, 1), (6, 1),),
+    ((2, 0), (3, 0), (1, 0),),
+    (),
+    ((9, 1),),
     (),
     (),
-    ((4, 3), (1, 2),),
-    ((2, 3), (5, 3), (3, 4),),
-    ((6, 2), (0, 1), (12, 0),),
+    ((3, 1), (4, 0),),
     (),
-    ((8, 0), (5, 4),),
+    ((2, 1), (9, 2),),
+    ((0, 0), (1, 1),),
+    ((3, 2), (2, 2),),
     (),
-    ((0, 2), (9, 0), (7, 0),),
+    ((9, 3), (4, 1),),
+    ((1, 2), (2, 3),),
+    ((0, 1), (3, 3),),
+    ((7, 0),),
+    ((9, 4), (5, 0), (1, 3), (4, 2), (6, 0),),
     (),
-    ((1, 3), (7, 1), (2, 4), (0, 3), (12, 1),),
-    ((4, 4), (12, 2),),
+    ((0, 2), (10, 0),),
     (),
-    ((8, 1), (8, 2), (13, 0), (7, 2), (10, 0), (11, 0), (6, 3), (9, 1), (12, 3), (2, 5), (13, 1), (0, 4), (6, 4), (1, 4), (7, 3), (13, 2), (8, 3), (5, 5), (9, 2),),
-    ((7, 4), (3, 5), (10, 1), (10, 2), (11, 1), (9, 3), (8, 4), (12, 4), (11, 2), (10, 3),),
     (),
-    ((9, 4),),
+    ((6, 1), (2, 4), (3, 4), (5, 1),),
+    ((10, 1), (4, 3),),
     (),
-    ((11, 3), (6, 5), (10, 4), (12, 5), (11, 4),),
-    ((4, 5),),
+    ((7, 1), (8, 0), (0, 3), (6, 2), (1, 4), (4, 4),),
+    ((10, 2), (5, 2), (7, 2), (8, 1), (0, 4),),
     (),
-    ((13, 3), (13, 4), (0, 5), (9, 5), (13, 5), (7, 5), (1, 5), (8, 5), (11, 5), (10, 5),),
+    (),
+    ((5, 3),),
+    ((10, 3), (5, 4), (8, 2), (7, 3), (7, 4), (9, 5), (8, 3), (6, 3), (10, 4), (10, 5),),
+    ((8, 4), (1, 5), (6, 4),),
+    (),
+    ((3, 5), (0, 5), (7, 5), (8, 5), (5, 5), (6, 5), (4, 5), (2, 5),),
 )
 
 
@@ -426,6 +426,72 @@
         self.save.wait()
 
 
+class ChunkG:
+    def __init__(self, sems, place, blocks, use=None):
+        def wires(query, device):
+            return [Wire(sems, block(query), block(query), device) for block in blocks]
+
+        self.place, self.use = place, use
+        first, second = place.far
+        self.pair = wires(place.query, place.pair)
+        self.x0 = wires(place.query, place.beside)
+        self.x1 = wires(place.pair[0], place.beside)
+        self.middle = wires(place.query, place.middle) + wires(place.pair[0], place.middle)
+        self.back = wires(first, place.pair) + wires(second, place.pair)
+        self.x2 = wires(first, place.beside) + wires(second, place.beside)
+
+    def s0(self):
+        for wire in self.pair + self.x0:
+            wire.start()
+
+    def s1(self):
+        for wire in self.pair:
+            wire.came()
+
+        @pl.when(self.place.inner)
+        def _():
+            for wire in self.middle:
+                wire.start()
+
+        for wire in self.x1:
+            wire.start()
+
+    def s2(self):
+        @pl.when(self.place.inner)
+        def _():
+            for wire in self.middle:
+                wire.came()
+            for wire in self.back + self.x2:
+                wire.start()
+
+    def s3(self):
+        @pl.when(self.place.end)
+        def _():
+            for wire in self.back:
+                wire.came()
+            for wire in self.x2:
+                wire.start()
+
+    def s4(self):
+        for wire in self.x0 + self.x1 + self.x2:
+            wire.came()
+
+    def s5(self):
+        self.saves = self.use()
+
+    def finish(self):
+        for wire in self.pair + self.x0 + self.x1 + self.x2:
+            wire.sent()
+
+        @pl.when(self.place.inner)
+        def _():
+            for wire in self.middle + self.back:
+                wire.sent()
+
+        for copy in self.saves:
+            copy.wait()
+
+
 class SmallSum:
     def __init__(self, sems, place, bufs):
         self.place = place
@@ -492,9 +558,8 @@
 
 
 def chunk_plan(own, width, units):
-    plan = [(0, k * (units // 2), units // 2) for k in range(2)]
-    plan += [(a, k * (width // 2), width // 2) for a in (1, 2) for k in range(2)]
-    plan += [(3, k * own, own) for k in range(8)]
+    plan = [(a, k * (width // 2), width // 2) for a in (1, 2) for k in range(2)]
+    plan += [(3, k * own, own) for k in (0, 1, 2, 6, 7)]
     return [(in_x, *block) for in_x, block in zip(IN_X, plan)]
 
 
@@ -504,7 +569,6 @@
         groups.append(SimpleNamespace(**jax.tree.unflatten(tree, refs[at : at + tree.num_leaves])))
         at += tree.num_leaves
     ins, outs, scr = groups
-    gain_self, gain_cross, gain_ffn = (gain[...].reshape(1, cfg.width) for gain in ins.gains)
     heads, all_heads, width, tokens, rows = cfg.heads, cfg.all_heads, cfg.width, cfg.tokens, cfg.rows
     own, pairs, tiles = heads * DH, all_heads // 2, rows // TILE
     summing = cfg.summing
@@ -530,6 +594,8 @@
         place.high = z // 2
         place.pair = ((z + 1 - 2 * lax.rem(z, 2)) * 2 + x, me)
         place.middle = ((3 - z) * 2 + x, me)
+        place.query = dp
+        place.far = ((2 - z // 2) * 2 + x, 3 * (1 - z // 2) * 2 + x)
         pl.semaphore_signal(barrier, inc=1, device_id=place.pair, device_id_type=MESH)
 
         @pl.when(inner)
@@ -542,17 +608,19 @@
         return copy
 
     enc, down, gate_w, up_w = scr.enc, scr.down, scr.gate_w, scr.up_w
-    first_loads = [fetch(ins.x, scr.x)]
+    first_loads = [fetch(ins.x, scr.x)] + [fetch(src, dst) for src, dst in zip(ins.gains, scr.gains)]
     self_weights = scr.wqkv
     for src, dst in zip((ins.wq_self, ins.wk_self, ins.wv_self), self_weights):
         first_loads.append(fetch(src, dst))
     load_bucket, load_out = fetch(ins.bucket, scr.bucket), fetch(ins.wo_self, scr.wo_self)
+    load_small = [fetch(ins.mask, scr.mask), fetch(ins.group, scr.group), fetch(ins.table, scr.table)]
     load_query = fetch(ins.wq_cross, scr.wq_own)
     load_enc = fetch(ins.encoder, enc)
     load_ffn = [fetch(ins.out_grad, scr.og), fetch(ins.down_w, down), fetch(ins.gate_w, gate_w), fetch(ins.up_w, up_w)]
 
     for load in first_loads:
         load.wait()
+    gain_self, gain_cross, gain_ffn = (gain[...].reshape(1, width) for gain in scr.gains)
     xv = scr.x[...].astype(F32)
     self_in = scr.self_in
     self_in[...] = (xv * rms_scale(xv) * gain_self).astype(BF)
@@ -569,14 +637,34 @@
         for part, whole in ((ins.wk_cross, wk), (ins.wq_cross, wq), (ins.wv_cross, wv), (ins.wo_cross, wo))
     ]
     get_k.start()
+    if summing:
+        lanes_half = span(core * (width // 2), width // 2, 2 * DH)
+        og_all, self_all, hidden_all, d_qkv_all = scr.gathered
+
+        def rows_of(query):
+            return span(query * tokens, tokens)
+
+        load_ffn[0].wait()
+        og_all[rows_of(dp), lanes_half] = scr.og[:, lanes_half]
+        self_all[rows_of(dp), lanes_half] = self_in[:, lanes_half]
+        early = ChunkG(
+            sems,
+            place,
+            [lambda query: og_all.at[rows_of(query), lanes_half], lambda query: self_all.at[rows_of(query), lanes_half]],
+            lambda: [],
+        )
+        shares = [Wire(sems, ref.at[:, lanes_half], ref.at[:, lanes_half], place.mate) for ref in (og_all, self_all)]
+        early.s0()
     load_bucket.wait()
+    for load in load_small:
+        load.wait()
     scr.bucket[...] = scr.bucket[...].T
     bucket = scr.bucket
-    keep = jnp.broadcast_to(ins.mask[...].astype(F32), (tokens, tokens)).T
+    keep = jnp.broadcast_to(scr.mask[...].astype(F32), (tokens, tokens)).T
     j_at = lax.broadcasted_iota(jnp.int32, (tokens, tokens), 0)
     i_at = lax.broadcasted_iota(jnp.int32, (tokens, tokens), 1)
     allowed = jnp.logical_or(jnp.logical_and(j_at <= i_at, keep == 1.0), j_at == i_at)
-    group = ins.group[0]
+    group = scr.group[0]
     buckets = cfg.buckets
     for h in range(heads):
         scr.p_self[h] = jnp.full((tokens, tokens), NEG, F32)
@@ -584,7 +672,7 @@
     def spread(b, _):
         hit = jnp.logical_and(bucket[...] == b, allowed)
         for h in range(heads):
-            scr.p_self[h] = jnp.where(hit, ins.table[h, group, b], scr.p_self[h])
+            scr.p_self[h] = jnp.where(hit, scr.table[h, group, b], scr.p_self[h])
         return 0
 
     lax.fori_loop(0, buckets, spread, 0)
@@ -612,16 +700,19 @@
     s1.one()
     s1.two()
     get_v.start()
+    bq, bw = scr.bq, scr.bw
+    for ref in (bq, bw, scr.stat, scr.top, scr.small[0], scr.bucket_rows):
+        ref[...] = jnp.zeros(ref.shape, ref.dtype)
     get_k.one()
     load_enc.wait()
+    if summing:
+        early.s1()
     kc, vc, e_ref = scr.kc, scr.vc, scr.e
 
-    def project(dst, weight, first, count):
-        lanes = span(first, count, 2 * DH)
-
+    def project(dst, weight):
         def body(r, _):
             at = span(r * TILE, TILE)
-            dst[at, lanes] = nt(enc[at], weight[lanes]).astype(BF)
+            dst[at] = nt(enc[at], weight[...]).astype(BF)
             return 0
 
         lax.fori_loop(0, tiles, body, 0)
@@ -641,18 +732,13 @@
     get_k.two()
     get_v.one()
     get_k.three()
-    project(kc, wk, 0, all_heads * DH)
+    project(kc, wk)
     get_query.two()
-    bq, bw = scr.bq, scr.bw
-    bq[...] = jnp.zeros(bq.shape, BF)
-    bw[...] = jnp.zeros(bw.shape, BF)
     get_query.three()
     for h in range(all_heads):
         at = slice(h * DH, (h + 1) * DH)
         bq[at, (h % 2) * tokens : (h % 2 + 1) * tokens] = scr.q_t[at]
     s_ref, mix, stat, top_ref = scr.s, scr.mix, scr.stat, scr.top
-    stat[...] = jnp.zeros(stat.shape, F32)
-    top_ref[...] = jnp.zeros(top_ref.shape, F32)
     per_half = pairs // 2
 
     def stat_row(p):
@@ -698,19 +784,21 @@
 
     lax.fori_loop(0, pairs - 2, score_pair, 0)
     get_v.two()
+    get_o.one()
+    if summing:
+        early.s2()
     lax.fori_loop(pairs - 2, pairs, score_pair, 0)
-    get_o.one()
     get_v.three()
     att, lse = scr.att, scr.lse
     s2 = TensorMix(sems, place, mix, stat, scr.mix_bufs, att, lse)
+    project(vc, wv)
     for half in (1 - core, core):
-        project(vc, wv, half * per_half * 2 * DH, per_half * 2 * DH)
         lax.fori_loop(half * per_half, (half + 1) * per_half, mix_pair, 0)
         if half is not core:
             s2.one()
             get_q.one()
     s2.two()
-    for load in load_ffn:
+    for load in load_ffn[1 if summing else 0 :]:
         load.wait()
     og = scr.og
     scr.d_hidden[...] = nt(og[...], down[...]).astype(BF).astype(F32)
@@ -718,6 +806,8 @@
     s2.three()
     get_o.three()
     s2.four()
+    if summing:
+        early.s3()
     x3 = scr.x3
     x3[...] = x2[...] + tn(att[...], wo[...])
     ffn_in = scr.ffn_in
@@ -735,12 +825,25 @@
     scr.d_gate[...] = (d_hidden * up * slope).astype(BF)
     scr.d_up[...] = (d_hidden * gelu).astype(BF)
 
+    g_down, g_gate, g_up, g_small = scr.grads
     chunks = []
     if summing:
+        def use_hidden():
+            g_down[...] = tn(hidden_all[...], og_all[...]).astype(BF)
+            return [fetch(g_down, outs.grads[0])]
+
+        def use_d_qkv():
+            whole = jnp.concatenate([d_qkv_all[k] for k in range(cfg.queries)], axis=1)
+            g_small[3 * own : 6 * own] = nn(whole, self_all[...]).astype(BF)
+            at = pl.ds(3 * own, 3 * own)
+            return [fetch(g_small.at[at], outs.grads[3].at[at])]
+
         for (in_x, source, start, size), bufs in zip(cfg.chunks, scr.chunks):
             rows_at = pl.ds(start, size)
             maker = ChunkX if in_x else ChunkZ
             chunks.append(maker(sems, place, scr.grads[source].at[rows_at], outs.grads[source].at[rows_at], bufs))
+        chunks.append(ChunkG(sems, place, [lambda query: hidden_all.at[rows_of(query)]], use_hidden))
+        chunks.append(ChunkG(sems, place, [lambda query: d_qkv_all.at[query]], use_d_qkv))
     schedule = iter(cfg.schedule)
 
     def poll():
@@ -749,8 +852,10 @@
                 chunk = chunks[n]
                 (chunk.s0, chunk.s1, chunk.s2, chunk.s3, chunk.s4, chunk.s5)[k]()
 
-    g_down, g_gate, g_up, g_small = scr.grads
-    g_down[...] = tn(scr.hidden[...], og[...]).astype(BF)
+    if summing:
+        hidden_all[rows_of(dp)] = scr.hidden[...]
+    else:
+        g_down[...] = tn(scr.hidden[...], og[...]).astype(BF)
     poll()
     g_gate[...] = tn(ffn_in[...], scr.d_gate[...]).astype(BF)
     poll()
@@ -774,7 +879,6 @@
     g2[...] = og[...].astype(F32) + dv
     g2_low[...] = g2[...].astype(BF)
     small = scr.small[0]
-    small[...] = jnp.zeros(small.shape, F32)
     small[2:3, :width] = gain_grad
     g_small[0:own] = nn(att[span(me * own, own)], g2_low[...]).astype(BF)
     poll()
@@ -838,6 +942,11 @@
         kv_half[a] = (far_parts[a][mine].astype(F32) + kv_near[a].astype(F32)).astype(BF)
         to_across[a].start()
 
+    if summing:
+        early.s4()
+        early.s5()
+        for wire in shares:
+            wire.start()
     for p in range(per_half):
         poll()
         lax.fori_loop(far_at + p, far_at + p + 1, backward_pair, 0)
@@ -845,6 +954,9 @@
     so.four()
     scr.out_stage[...] = (x3[...] + so.out[...].astype(F32)).astype(BF)
     token_saves = [fetch(scr.out_stage, outs.block_out)]
+    if summing:
+        for wire in shares:
+            wire.came()
     weight_part(far_parts[0], kc, far_at)
     to_mate[0].start()
     weight_part(far_parts[1], vc, far_at)
@@ -899,7 +1011,10 @@
         d_qkv[own + h * DH : own + (h + 1) * DH] = nt(q, ds).astype(BF)
         d_qkv[2 * own + h * DH : 2 * own + (h + 1) * DH] = nt(d_att_self[at], p.astype(BF)).astype(BF)
     poll()
-    g_small[3 * own : 6 * own] = nn(d_qkv[...], self_in[...]).astype(BF)
+    if summing:
+        d_qkv_all[dp] = d_qkv[...]
+    else:
+        g_small[3 * own : 6 * own] = nn(d_qkv[...], self_in[...]).astype(BF)
     poll()
     s5 = tensor_sum(scr.s5)
     total = None
@@ -919,7 +1034,6 @@
         return 0
 
     s5.two()
-    rows_ref[...] = jnp.zeros(rows_ref.shape, F32)
     lax.fori_loop(0, buckets, count, 0)
     position = jnp.sum(rows_ref[...].T, axis=0, keepdims=True)
     for g in range(cfg.groups):
@@ -965,14 +1079,17 @@
         little.s3()
         poll()
         little.s4()
-        outs.small_sum[...] = little.bufs[6][...]
+        last = fetch(little.bufs[6], outs.small_sum)
         poll()
-        for chunk in chunks:
+        for chunk in chunks + [early]:
             chunk.finish()
+        for wire in shares:
+            wire.sent()
     else:
         for copy in [fetch(src, dst) for src, dst in zip(scr.grads, outs.grads)]:
             copy.wait()
-        outs.small_sum[...] = small[...]
+        last = fetch(small, outs.small_sum)
+    last.wait()
     for gather in gathers + [get_query]:
         gather.end()
 
@@ -1052,10 +1169,10 @@
         x=(decoder_in[0], ANY),
         out_grad=(out_grad[0], ANY),
         encoder=(encoder_out[0], ANY),
-        group=(group_ids, SMEM),
-        mask=(target_mask, VMEM),
+        group=(group_ids, ANY),
+        mask=(target_mask, ANY),
         bucket=(bucket_ids, ANY),
-        gains=[(gain_self, VMEM), (gain_cross, VMEM), (gain_ffn, VMEM)],
+        gains=[(gain_self, ANY), (gain_cross, ANY), (gain_ffn, ANY)],
         wq_self=(query_self.T, ANY),
         wk_self=(key_self.T, ANY),
         wv_self=(value_self.T, ANY),
@@ -1067,7 +1184,7 @@
         gate_w=(gate_weight, ANY),
         up_w=(up_weight, ANY),
         down_w=(down_weight, ANY),
-        table=(jnp.transpose(position_bias, (2, 0, 1)), SMEM),
+        table=(jnp.transpose(position_bias, (2, 0, 1)), ANY),
     )
     grad_shapes = [(units, width), (width, units), (width, units), (8 * own, width)]
     outputs = dict(
@@ -1075,7 +1192,7 @@
         decoder_grad=(shape_of(tokens, width), ANY),
         encoder_grad=(shape_of(rows, width), ANY),
         grads=[(shape_of(*shape), ANY) for shape in grad_shapes],
-        small_sum=(shape_of(16, width, kind=F32), VMEM),
+        small_sum=(shape_of(16, width, kind=F32), ANY),
     )
     plan = chunk_plan(own, width, units)
     all_own = all_heads * DH
@@ -1092,6 +1209,8 @@
     stats, kv_block = vmem(16, tokens, kind=F32), vmem(2, own, width)
     halves = vmem(all_own // 2, tokens)
     scratch = dict(
+        gains=[vmem(width, kind=F32)] * 3, mask=vmem(1, tokens, kind=jnp.int32),
+        group=pltpu.SMEM((1,), jnp.int32), table=pltpu.SMEM((heads, groups, buckets), F32),
         x=token_low, og=token_low, out_stage=token_low, wqkv=[vmem(own, width)] * 3, wo_self=vmem(own, width), wq_own=vmem(own, width),
         q_own=vmem(own, tokens), q_t=vmem(all_own, tokens),
         enc=vmem(rows, width), down=vmem(units, width), gate_w=vmem(width, units), up_w=vmem(width, units),
@@ -1116,8 +1235,10 @@
         stage=vmem(2, TILE, width),
         grads=[vmem(*shape) for shape in grad_shapes],
         small=[vmem(16, width, kind=F32)] * (7 if summing else 1),
+        gathered=[vmem(dp_size * tokens, width)] * 2
+        + [vmem(dp_size * tokens, units), vmem(dp_size, 3 * own, tokens)] if summing else [],
         chunks=[chunk_bufs(in_x, source, size) for in_x, source, _, size in plan] if summing else [],
-        sems=pltpu.SemaphoreType.DMA((320,)),
+        sems=pltpu.SemaphoreType.DMA((400,)),
     )
     pair = lambda entry: isinstance(entry, tuple)
     first = lambda tree: jax.tree.map(lambda entry: entry[0], tree, is_leaf=pair)
@@ -1126,7 +1247,7 @@
     trees = [jax.tree.structure(first(inputs)), jax.tree.structure(first(outputs)), jax.tree.structure(scratch)]
     cfg = SimpleNamespace(
         trees=trees, heads=heads, all_heads=all_heads, width=width, tokens=tokens, rows=rows,
-        buckets=buckets, groups=groups, summing=summing, chunks=plan, schedule=SCHEDULE,
+        buckets=buckets, groups=groups, queries=dp_size, summing=summing, chunks=plan, schedule=SCHEDULE,
     )
     result = pl.pallas_call(
         functools.partial(block_kernel, cfg),

time: 157 us -> 145 us (0.924)
  Pallas kernels: 155 us -> 143 us
    pallas_call x1, Pallas kernels: 147 us -> 135 us  [shards(): pl.pallas_call(functools.partial(block_kernel, cfg), out_shape=flat(first...]
where the time goes in v4:
time: 145 us
  Pallas kernels  143 us (99%)
  between operations  1.5 us (1%)
    pallas_call x1, Pallas kernels, shards(): pl.pallas_call(functools.partial(block_kernel, cfg), out_shape=flat(first...  135 us
    pallas_call x1, Pallas kernels, shards(): pl.pallas_call(finish, out_shape=flat(outputs), in_specs=flat(specs_in),...  8.67 us

profile of v4, /device:TPU:0, one launch (start us, length us, event | category | flops | bytes accessed | tf_op | source)
XLA Modules:
  0.0 144.7 jit_solution(2948324545448265293)
XLA Ops:
  1.3 134.5 %block.1 = (bf16[128,768]{1,0:T(8,128)(2,1)}, bf16[128,768]{1,0:T(8,128)(2,1)}, bf16[1536,768]{1,0:T(8,128)(2,1)}, bf16[512,768]{1,0:T(8,128)(2,1)}, bf16[768,51...) custom-call(s32[128,128]{1,0:T(8,128)} %refs_0_.1, ...), custom_call_target="tpu_custom_call" | custom-call | tf_op jit(solution)/shard_map/block/pallas_call | solution.py:1252
  135.8 8.7 %finish.1 = (f32[768]{0:T(1024)}, f32[768]{0:T(1024)}, f32[768]{0:T(1024)}, bf16[128,768]{1,0:T(8,128)(2,1)}, bf16[128,768]{1,0:T(8,128)(2,1)}, /*index=5*/bf16[...) custom-call(bf16[512,768]{1,0:T(8,128)(2,1)} %get-tuple-element.44.r, ...), custom_call_target="tpu_custom_call" | custom-call | tf_op jit(solution)/shard_map/finish/pallas_call | solution.py:1289

commit v5 on v4

--- a/solution.py
+++ b/solution.py
@@ -22,43 +22,43 @@
 GELU_CUBIC = 0.044715
 
 
-IN_X = (True, True, True, False, True, True, False, True, True)
+IN_X = (True, True, True, True, False, False, True, True, True)
 SCHEDULE = (
-    ((9, 0),),
     (),
     (),
-    ((2, 0), (3, 0), (1, 0),),
+    ((1, 0),),
+    ((9, 0), (2, 0), (3, 0),),
+    ((0, 0),),
     (),
+    (),
+    (),
+    ((4, 0),),
     ((9, 1),),
     (),
     (),
-    ((3, 1), (4, 0),),
+    ((1, 1),),
+    ((4, 1), (9, 2),),
+    ((3, 1),),
+    ((9, 3), (1, 2), (4, 2),),
     (),
-    ((2, 1), (9, 2),),
-    ((0, 0), (1, 1),),
-    ((3, 2), (2, 2),),
-    (),
-    ((9, 3), (4, 1),),
-    ((1, 2), (2, 3),),
-    ((0, 1), (3, 3),),
-    ((7, 0),),
-    ((9, 4), (5, 0), (1, 3), (4, 2), (6, 0),),
-    (),
-    ((0, 2), (10, 0),),
+    ((7, 0), (3, 2), (0, 1), (1, 3),),
     (),
     (),
-    ((6, 1), (2, 4), (3, 4), (5, 1),),
-    ((10, 1), (4, 3),),
+    ((10, 0), (4, 3),),
+    ((0, 2), (5, 0), (7, 1), (6, 0), (3, 3),),
     (),
-    ((7, 1), (8, 0), (0, 3), (6, 2), (1, 4), (4, 4),),
-    ((10, 2), (5, 2), (7, 2), (8, 1), (0, 4),),
+    ((10, 1),),
     (),
+    ((0, 3), (1, 4),),
+    ((8, 0), (6, 1), (2, 1), (3, 4),),
+    ((5, 1), (10, 2),),
+    ((0, 4), (4, 4), (6, 2),),
+    ((7, 2),),
+    ((2, 2), (3, 5), (8, 1), (6, 3), (5, 2), (7, 3), (10, 3), (8, 2),),
+    ((9, 4), (2, 3), (6, 4), (10, 4), (7, 4), (8, 3), (5, 3), (2, 4), (8, 4), (1, 5), (10, 5),),
+    ((5, 4), (9, 5), (7, 5), (0, 5), (6, 5),),
     (),
-    ((5, 3),),
-    ((10, 3), (5, 4), (8, 2), (7, 3), (7, 4), (9, 5), (8, 3), (6, 3), (10, 4), (10, 5),),
-    ((8, 4), (1, 5), (6, 4),),
-    (),
-    ((3, 5), (0, 5), (7, 5), (8, 5), (5, 5), (6, 5), (4, 5), (2, 5),),
+    ((2, 5), (4, 5), (5, 5), (8, 5),),
 )
 
 

time: 145 us -> 138 us (0.952)
  Pallas kernels: 143 us -> 137 us
    pallas_call x1, Pallas kernels: 135 us -> 128 us  [shards(): pl.pallas_call(functools.partial(block_kernel, cfg), out_shape=flat(first...]
where the time goes in v5:
time: 138 us
  Pallas kernels  137 us (99%)
  between operations  1.5 us (1%)
    pallas_call x1, Pallas kernels, shards(): pl.pallas_call(functools.partial(block_kernel, cfg), out_shape=flat(first...  128 us
    pallas_call x1, Pallas kernels, shards(): pl.pallas_call(finish, out_shape=flat(outputs), in_specs=flat(specs_in),...  8.67 us

profile of v5, /device:TPU:0, one launch (start us, length us, event | category | flops | bytes accessed | tf_op | source)
XLA Modules:
  0.0 138.2 jit_solution(7893723985300764672)
XLA Ops:
  1.3 128.0 %block.1 = (bf16[128,768]{1,0:T(8,128)(2,1)}, bf16[128,768]{1,0:T(8,128)(2,1)}, bf16[1536,768]{1,0:T(8,128)(2,1)}, bf16[512,768]{1,0:T(8,128)(2,1)}, bf16[768,51...) custom-call(s32[128,128]{1,0:T(8,128)} %refs_0_.1, ...), custom_call_target="tpu_custom_call" | custom-call | tf_op jit(solution)/shard_map/block/pallas_call | solution.py:1252
  129.3 8.7 %finish.1 = (f32[768]{0:T(1024)}, f32[768]{0:T(1024)}, f32[768]{0:T(1024)}, bf16[128,768]{1,0:T(8,128)(2,1)}, bf16[128,768]{1,0:T(8,128)(2,1)}, /*index=5*/bf16[...) custom-call(bf16[512,768]{1,0:T(8,128)(2,1)} %get-tuple-element.44.r, ...), custom_call_target="tpu_custom_call" | custom-call | tf_op jit(solution)/shard_map/finish/pallas_call | solution.py:1289

commit v6 on v5

--- a/solution.py
+++ b/solution.py
@@ -26,39 +26,39 @@
 SCHEDULE = (
     (),
     (),
-    ((1, 0),),
-    ((9, 0), (2, 0), (3, 0),),
-    ((0, 0),),
-    (),
-    (),
+    ((2, 0), (9, 0),),
+    (),
+    ((1, 0), (3, 0), (0, 0),),
     (),
     ((4, 0),),
+    (),
+    (),
     ((9, 1),),
     (),
     (),
-    ((1, 1),),
-    ((4, 1), (9, 2),),
+    ((4, 1), (9, 2), (1, 1),),
     ((3, 1),),
+    (),
     ((9, 3), (1, 2), (4, 2),),
     (),
-    ((7, 0), (3, 2), (0, 1), (1, 3),),
+    ((7, 0), (0, 1), (3, 2), (1, 3),),
     (),
     (),
     ((10, 0), (4, 3),),
-    ((0, 2), (5, 0), (7, 1), (6, 0), (3, 3),),
-    (),
-    ((10, 1),),
-    (),
-    ((0, 3), (1, 4),),
-    ((8, 0), (6, 1), (2, 1), (3, 4),),
-    ((5, 1), (10, 2),),
-    ((0, 4), (4, 4), (6, 2),),
+    ((5, 0), (0, 2), (7, 1), (6, 0), (3, 3),),
+    (),
+    ((1, 4), (10, 1),),
+    (),
+    ((0, 3),),
+    ((8, 0), (3, 4), (6, 1), (2, 1),),
+    ((5, 1), (0, 4), (10, 2),),
+    ((4, 4), (6, 2),),
     ((7, 2),),
-    ((2, 2), (3, 5), (8, 1), (6, 3), (5, 2), (7, 3), (10, 3), (8, 2),),
-    ((9, 4), (2, 3), (6, 4), (10, 4), (7, 4), (8, 3), (5, 3), (2, 4), (8, 4), (1, 5), (10, 5),),
-    ((5, 4), (9, 5), (7, 5), (0, 5), (6, 5),),
-    (),
-    ((2, 5), (4, 5), (5, 5), (8, 5),),
+    ((2, 2), (5, 2), (6, 3), (3, 5), (8, 1), (7, 3), (10, 3), (8, 2), (2, 3),),
+    ((6, 4), (8, 3), (7, 4), (10, 4), (2, 4), (5, 3), (1, 5), (9, 4), (6, 5), (8, 4), (10, 5),),
+    ((4, 5), (5, 4), (9, 5), (7, 5),),
+    (),
+    ((0, 5), (2, 5), (5, 5), (8, 5),),
 )
 
 

time: 138 us -> 137 us (level)
  no operation moved by 1% of the time
where the time goes in v6:
time: 137 us
  Pallas kernels  136 us (99%)
  between operations  1.5 us (1%)
    pallas_call x1, Pallas kernels, shards(): pl.pallas_call(functools.partial(block_kernel, cfg), out_shape=flat(first...  127 us
    pallas_call x1, Pallas kernels, shards(): pl.pallas_call(finish, out_shape=flat(outputs), in_specs=flat(specs_in),...  8.67 us

profile of v6, /device:TPU:0, one launch (start us, length us, event | category | flops | bytes accessed | tf_op | source)
XLA Modules:
  0.0 137.0 jit_solution(10979289835033299535)
XLA Ops:
  1.3 126.9 %block.1 = (bf16[128,768]{1,0:T(8,128)(2,1)}, bf16[128,768]{1,0:T(8,128)(2,1)}, bf16[1536,768]{1,0:T(8,128)(2,1)}, bf16[512,768]{1,0:T(8,128)(2,1)}, bf16[768,51...) custom-call(s32[128,128]{1,0:T(8,128)} %refs_0_.1, ...), custom_call_target="tpu_custom_call" | custom-call | tf_op jit(solution)/shard_map/block/pallas_call | solution.py:1252
  128.2 8.7 %finish.1 = (f32[768]{0:T(1024)}, f32[768]{0:T(1024)}, f32[768]{0:T(1024)}, bf16[128,768]{1,0:T(8,128)(2,1)}, bf16[128,768]{1,0:T(8,128)(2,1)}, /*index=5*/bf16[...) custom-call(bf16[512,768]{1,0:T(8,128)(2,1)} %get-tuple-element.44.r, ...), custom_call_target="tpu_custom_call" | custom-call | tf_op jit(solution)/shard_map/finish/pallas_call | solution.py:1289
